TPU v7x, 32 devices: a whole 2x2x4 slice. The times are simulated.
32 devices in a mesh: rows: 16 (over z, x, core), feat: 2 (over y).
Axes of the slice: x: 2, y: 2, z: 4, core: 2. Of those that a mesh axis runs over, the one named last changes fastest.
Arguments:
- gradients: bfloat16 [16384, 8192], P('rows', 'feat'), may hold values from -2500 to 2500
- queries: bfloat16 [1024, 8192], P('rows', 'feat'), may hold values from -0.09375 to 0.09375
- loss_weight: float32 [16384], P('rows'), may hold values from 0.09 to 1
Outputs:
- standardized: bfloat16 [16384, 1024], P('rows', 'feat')
All inputs are finite; a program needn't handle non-finite values.
Results may differ from a plain program's by a relative error of at most 0.019.
Values may be sent and summed in bfloat16 or wider, within the bound.
No kernel may reach another device: no remote copies, remote signals or barrier semaphores. Data moves between devices by JAX's collectives and lax.ppermute only.
A program may use at most 64 MiB of HBM per device.

v0:
```python
import functools

import jax
import jax.numpy as jnp
from jax import lax
from jax.experimental import pallas as pl
from jax.experimental.pallas import tpu as pltpu
from jax.sharding import PartitionSpec as P


NORM_EPS = 1e-06
VAR_EPS = 1e-05
VMEM = pl.BlockSpec(memory_space=pltpu.VMEM)
NT = (((1,), (1,)), ((), ()))


def plain_body(gradients, queries, loss_weight):
    rows_here = gradients.shape[0]
    total_rows = rows_here * lax.axis_size("rows")
    feature_count = gradients.shape[1] * lax.axis_size("feat")
    local_squares = jnp.sum(jnp.square(gradients.astype(jnp.float32)), axis=1)
    squares = lax.psum(local_squares, "feat")
    product = lax.dot_general(
        gradients,
        lax.all_gather(queries, "rows", axis=0, tiled=True),
        NT,
        preferred_element_type=jnp.float32,
    )
    raw = lax.psum_scatter(
        product.astype(jnp.bfloat16), "feat", scatter_dimension=1, tiled=True
    ).astype(jnp.float32)
    factor = loss_weight / jnp.sqrt(squares / feature_count + NORM_EPS)
    scored = raw * factor[:, None]
    column_mean = lax.psum(jnp.sum(scored, axis=0), "rows") / total_rows
    centered = scored - column_mean[None, :]
    square_sums = lax.psum(jnp.sum(centered * centered, axis=0), "rows")
    column_var = square_sums / total_rows
    return (centered * lax.rsqrt(column_var + VAR_EPS)[None, :]).astype(jnp.bfloat16)


def ring_order(planes):
    return [(z, 0) for z in range(planes)] + [(z, 1) for z in range(planes - 1, -1, -1)]


class Plan:
    def __init__(self, planes):
        self.order = ring_order(planes)
        self.nodes = len(self.order)
        self.far = self.nodes // 2
        low, high = [0], [0]
        for s in range(1, self.far):
            low += [-s, s]
            high += [s, -s]
        self.offsets = (low + [self.far], high + [self.far])
        self.pairs = len(self.offsets[0])
        self.turns = self.pairs // 2
        self.give, self.take, self.place = {}, {}, {}
        for n, (z, x) in enumerate(self.order):
            for f in range(2):
                key = (z * 2 + x) * 2 + f
                for half in range(2):
                    mine, other = [], []
                    spot = [0] * self.turns
                    for p, o in enumerate(self.offsets[half]):
                        oz, ox = self.order[(n + o) % self.nodes]
                        chip = oz * 2 + ox
                        if chip // self.turns == f:
                            spot[chip % self.turns] = len(mine)
                            mine.append(p)
                        else:
                            other.append(p)
                    self.give[key, half] = other
                    self.take[key, half] = mine
                    self.place[key, half] = spot

    def packed(self, table, half):
        key = (lax.axis_index("rows") // 2) * 2 + lax.axis_index("feat")
        codes = [sum(v << (4 * m) for m, v in enumerate(table[k, half])) for k in range(2 * self.nodes)]
        code = jnp.int32(codes[0])
        for k in range(1, 2 * self.nodes):
            code = jnp.where(key == k, jnp.int32(codes[k]), code)
        return code

    def options(self, table, half, m):
        return sorted({table[k, half][m] for k in range(2 * self.nodes)})


def entry(code, m):
    return (code >> (4 * m)) & 15


def gather_block(plan, table, m, blocks, held):
    for half in range(2):
        index = entry(plan.packed(table, half), m)
        for p in plan.options(table, half, m):
            @pl.when(index == p)
            def _(half=half, p=p):
                held[half] = blocks[p]()
    lane = lax.broadcasted_iota(jnp.int32, held.shape[1:], 1)
    return jnp.where(lane < held.shape[2] // 2, held[0], held[1])


def product_kernel(plan, sources, count, turn, known, grad_ref, *refs):
    units, refs = refs[:count], refs[count:]
    older, refs = refs[:len(known)], refs[len(known):]
    out_ref, refs = refs[0], refs[2:]
    if turn is not None:
        send_ref, held, pick = refs
    else:
        (held,) = refs
    shard = units[0].shape[0]
    core = lax.axis_index("rows") % 2
    for k in range(count):
        pair, same = k // 2, sources[k]
        spot = pair * 2 + (core if same else 1 - core)
        held[pl.ds(pl.multiple_of(spot * shard, shard), shard), :] = units[k][...]
    product = lax.dot_general(grad_ref[...], held[...], NT, preferred_element_type=jnp.float32)
    for b in range(out_ref.shape[0]):
        out_ref[b] = product[:, b * 128:(b + 1) * 128].astype(jnp.bfloat16)
    if turn is not None:
        blocks = block_readers(known, older)
        first = sum(n for n, _ in known) if known else 0
        for b in range(out_ref.shape[0]):
            blocks[first + b] = lambda b=b: out_ref[b]
        send_ref[...] = gather_block(plan, plan.give, turn, blocks, pick)


def block_readers(known, refs):
    blocks, p = {}, 0
    for (n, _), ref in zip(known, refs):
        for b in range(n):
            blocks[p] = lambda ref=ref, b=b: ref[b]
            p += 1
    return blocks


def product_call(plan, gradients, units, sources, known=(), turn=None):
    rows, depth = gradients.shape
    shard = units[0].shape[0]
    count = len(units)
    n = count // 2
    out_shape = [
        jax.ShapeDtypeStruct((n, rows, 128), jnp.bfloat16),
        jax.ShapeDtypeStruct(gradients.shape, gradients.dtype),
    ]
    scratch = [pltpu.VMEM((count * shard, depth), jnp.bfloat16)]
    if turn is None:
        known = ()
    else:
        out_shape.append(jax.ShapeDtypeStruct((rows, 128), jnp.bfloat16))
        scratch.append(pltpu.VMEM((2, rows, 128), jnp.bfloat16))
    known = list(known)
    return pl.pallas_call(
        functools.partial(product_kernel, plan, sources, count, turn, known),
        out_shape=out_shape,
        in_specs=[VMEM] * (1 + count + len(known)),
        out_specs=[VMEM] * len(out_shape),
        scratch_shapes=scratch,
        input_output_aliases={0: 1},
        compiler_params=pltpu.CompilerParams(vmem_limit_bytes=12 * 1024 * 1024),
        cost_estimate=pl.CostEstimate(
            flops=2 * rows * depth * count * shard, bytes_accessed=2 * rows * depth, transcendentals=0
        ),
    )(gradients, *units, *[a for _, a in known])


def load_kernel(parts, grad_ref, held_ref, square_ref, sem):
    rows, depth = held_ref.shape
    piece = rows // parts
    copies = [
        pltpu.make_async_copy(grad_ref.at[pl.ds(k * piece, piece)], held_ref.at[pl.ds(k * piece, piece)], sem.at[k])
        for k in range(parts)
    ]
    for copy in copies:
        copy.start()
    for k, copy in enumerate(copies):
        copy.wait()

        def step(i, carry, k=k):
            here = pl.ds(pl.multiple_of(k * piece + i * 64, 64), 64)
            total = jnp.zeros((64, 128), jnp.float32)
            for c in range(depth // 128):
                wide = held_ref[here, c * 128:(c + 1) * 128].astype(jnp.float32)
                total = total + wide * wide
            square_ref[here, :] = jnp.sum(total, axis=1, keepdims=True)
            return carry

        lax.fori_loop(0, piece // 64, step, 0)


def load_call(gradients, parts=4):
    rows, depth = gradients.shape
    return pl.pallas_call(
        functools.partial(load_kernel, parts),
        out_shape=[
            jax.ShapeDtypeStruct((rows, depth), gradients.dtype),
            jax.ShapeDtypeStruct((rows, 1), jnp.float32),
        ],
        in_specs=[pl.BlockSpec(memory_space=pltpu.HBM)],
        out_specs=[VMEM, VMEM],
        scratch_shapes=[pltpu.SemaphoreType.DMA((parts,))],
        compiler_params=pltpu.CompilerParams(vmem_limit_bytes=8 * 1024 * 1024),
        cost_estimate=pl.CostEstimate(flops=2 * rows * depth, bytes_accessed=2 * rows * depth, transcendentals=0),
    )(pltpu.with_memory_space_constraint(gradients, pltpu.HBM))


def score_kernel(plan, turns, known, first, depth, *refs):
    comes, refs = refs[:len(turns)], refs[len(turns):]
    if first:
        square_ref, other_ref, weight_ref, refs = *refs[:3], refs[3:]
    else:
        factor_ref, before_ref, refs = *refs[:2], refs[2:]
    older, refs = refs[:len(known)], refs[len(known):]
    if first:
        scored_ref, stat_ref, factor_ref, pick = refs
        eye = lax.broadcasted_iota(jnp.int32, (128, 128), 0) == lax.broadcasted_iota(jnp.int32, (128, 128), 1)
        for i in range(weight_ref.shape[0]):
            rows = slice(i * 128, (i + 1) * 128)
            weight = jnp.sum(jnp.where(eye, weight_ref[i:i + 1, :], 0.0), axis=1, keepdims=True)
            squares = square_ref[rows, :] + other_ref[rows, :]
            factor_ref[rows, :] = weight / jnp.sqrt(squares / depth + NORM_EPS)
    else:
        scored_ref, stat_ref, pick = refs
    blocks = block_readers(known, older)
    stats = []
    for b, turn in enumerate(turns):
        keep = gather_block(plan, plan.take, turn, blocks, pick)
        raw = keep.astype(jnp.float32) + comes[b][...].astype(jnp.float32)
        scored = raw * factor_ref[...]
        scored_ref[b] = scored
        mean = jnp.sum(scored, axis=0, keepdims=True) / scored.shape[0]
        centered = scored - mean
        both = jnp.concatenate([mean, jnp.sum(centered * centered, axis=0, keepdims=True)], axis=0)
        if first:
            stat_ref[b] = both
        else:
            stats.append(both)
    if not first:
        stats = [before_ref[b] for b in range(before_ref.shape[0])] + stats
        lane = lax.broadcasted_iota(jnp.int32, (2, 128), 1)
        codes = [plan.packed(plan.place, half) for half in range(2)]
        for j in range(plan.turns):
            halves = []
            for half in range(2):
                index = entry(codes[half], j)
                value = stats[0]
                for m in range(1, len(stats)):
                    value = jnp.where(index == m, stats[m], value)
                halves.append(value)
            stat_ref[:, j * 128:(j + 1) * 128] = jnp.where(lane < 64, halves[0], halves[1])


def score_call(plan, turns, comes, known, depth, squares=None, factor=None, before=None):
    rows = comes[0].shape[0]
    first = squares is not None
    n = len(turns)
    stat = (n, 2, 128) if first else (2, plan.turns * 128)
    args = list(comes) + (list(squares) if first else [factor, before]) + [a for _, a in known]
    out_shape = [jax.ShapeDtypeStruct((n, rows, 128), jnp.float32), jax.ShapeDtypeStruct(stat, jnp.float32)]
    if first:
        out_shape.append(jax.ShapeDtypeStruct((rows, 1), jnp.float32))
    return pl.pallas_call(
        functools.partial(score_kernel, plan, turns, known, first, depth),
        out_shape=out_shape,
        in_specs=[VMEM] * len(args),
        out_specs=[VMEM] * len(out_shape),
        scratch_shapes=[pltpu.VMEM((2, rows, 128), jnp.bfloat16)],
        compiler_params=pltpu.CompilerParams(vmem_limit_bytes=8 * 1024 * 1024),
        cost_estimate=pl.CostEstimate(flops=8 * n * rows * 128, bytes_accessed=12 * n * rows * 128, transcendentals=0),
    )(*args)


def finish_kernel(plan, count, stat_ref, early_ref, late_ref, out_ref):
    lane = lax.broadcasted_iota(jnp.int32, late_ref.shape[1:], 1)
    codes = [plan.packed(plan.place, half) for half in range(2)]
    early = early_ref.shape[0]
    scale = lax.rsqrt(stat_ref[1:2, :] / count + VAR_EPS)
    for j in range(plan.turns):
        halves = []
        for half in range(2):
            index = entry(codes[half], j)
            value = early_ref[jnp.minimum(index, early - 1)]
            halves.append(jnp.where(index < early, value, late_ref[0]))
        value = jnp.where(lane < 64, halves[0], halves[1])
        columns = slice(j * 128, (j + 1) * 128)
        out_ref[:, columns] = ((value - stat_ref[0:1, columns]) * scale[:, columns]).astype(jnp.bfloat16)


def finish_call(plan, count, stat, early, late):
    rows = late.shape[1]
    width = plan.turns * 128
    return pl.pallas_call(
        functools.partial(finish_kernel, plan, count),
        out_shape=jax.ShapeDtypeStruct((rows, width), jnp.bfloat16),
        in_specs=[VMEM] * 3,
        out_specs=VMEM,
        compiler_params=pltpu.CompilerParams(vmem_limit_bytes=8 * 1024 * 1024),
        cost_estimate=pl.CostEstimate(flops=2 * rows * width, bytes_accessed=6 * rows * width, transcendentals=0),
    )(stat, early, late)


def product_groups(plan):
    groups, p, m = [], 0, 0
    while p < plan.pairs:
        ready = max(max(plan.options(plan.give, half, m)) for half in range(2))
        n = 2 if p + 1 < ready and p + 1 < plan.pairs else 1
        done = p + n > ready
        groups.append((p, n, m if done else None))
        m += done
        p += n
    return groups


def ring_body(planes, gradients, queries, loss_weight):
    plan = Plan(planes)
    nodes, far = plan.nodes, plan.far
    rows_here, depth = gradients.shape
    feature_count = depth * 2

    def device(node, c):
        z, x = plan.order[node % nodes]
        return (z * 2 + x) * 2 + c

    swap = [(r, r ^ 1) for r in range(2 * nodes)]
    turn = [(device(n, 0), device(n + 1, 0)) for n in range(nodes)]
    turn += [(device(n, 1), device(n - 1, 1)) for n in range(nodes)]

    def cross(value):
        return lax.ppermute(value, "feat", [(0, 1), (1, 0)])

    ring = [queries, lax.ppermute(queries, "rows", swap)]
    for _ in range(1, 2 * far):
        ring.append(lax.ppermute(ring[-2], "rows", turn))
    arrived = [([queries, ring[1]], [True, False])]
    for k in range(1, 2 * far):
        arrived.append(([ring[k + 1], lax.ppermute(ring[k + 1], "rows", swap)], [k % 2 == 1, k % 2 == 0]))

    gradients, squares = load_call(gradients)
    squares = (squares, cross(squares), loss_weight.reshape(rows_here // 128, 128))

    known, comes = [], []
    for p, n, m in product_groups(plan):
        units, sources = [], []
        for u, s in arrived[p:p + n]:
            units, sources = units + u, sources + s
        out = product_call(plan, gradients, units, sources, known, m)
        known.append((n, out[0]))
        if m is not None:
            comes.append(cross(out[2]))
        gradients = out[1]
    last = len(comes) - 1
    early, stat, factor = score_call(plan, list(range(last)), comes[:last], known, feature_count, squares)
    late, stat = score_call(plan, [last], comes[last:], known, feature_count, None, factor, stat)

    mean, spread = stat[0:1], stat[1:2]
    count, step = rows_here, 1
    while step < 2 * nodes:
        pairs = [(r, r ^ step) for r in range(2 * nodes)]
        come = lax.ppermute(jnp.concatenate([mean, spread], axis=0), "rows", pairs)
        gap = come[0:1] - mean
        mean = 0.5 * (mean + come[0:1])
        spread = spread + come[1:2] + (0.5 * count) * (gap * gap)
        count *= 2
        step *= 2
    return finish_call(plan, count, jnp.concatenate([mean, spread], axis=0), early, late)


def solution(mesh):
    in_specs = (P("rows", "feat"), P("rows", "feat"), P("rows"))
    out_specs = P("rows", "feat")
    rows, feat = mesh.shape["rows"], mesh.shape["feat"]
    planes = rows // 4
    fits = rows == 4 * planes and planes in (2, 4) and feat == 2

    def body(gradients, queries, loss_weight):
        if fits and 2 * queries.shape[0] == 128 and gradients.shape[0] % 256 == 0:
            return ring_body(planes, gradients, queries, loss_weight)
        return plain_body(gradients, queries, loss_weight)

    return jax.shard_map(body, mesh=mesh, in_specs=in_specs, out_specs=out_specs, check_vma=False)
```

profile of v0, /device:TPU:0, one launch (start us, length us, event | category | flops | bytes accessed | tf_op | source)
XLA Modules:
  0.0 108.0 jit_solution(1656196413166537112)
XLA Ops:
  0.0 0.0 copy-start
  0.0 0.5 collective-permute-start
  0.5 2.6 %collective-permute-start.1 = (bf16[64,4096]{1,0:T(8,128)(2,1)}, bf16[64,4096]{1,0:T(8,128)(2,1)S(1)}, u32[]{:S(2)}, u32[]{:S(2)}) collective-permute-start(bf16[64,4096]{1,0:T(8,128)(2,1)} %refs_0_.1), channel_id=1, source_target_pairs={{0,8},{8,16},{16,24},{24,28},{28,20},{20,12},{12,4},{4,0},{2,6},{1... | collective-permute-start | bytes 1572872 | tf_op jit(solution)/shard_map/ppermute | solution.py:333
  3.1 0.0 collective-permute-done.refs_1_
  3.1 2.1 %collective-permute-start.3 = (bf16[64,4096]{1,0:T(8,128)(2,1)S(1)}, bf16[64,4096]{1,0:T(8,128)(2,1)S(1)}, u32[]{:S(2)}, u32[]{:S(2)}) collective-permute-start(bf16[64,4096]{1,0:T(8,128)(2,1)S(1)} %collective-permute-done.refs_1_), channel_id=1, source_target_pairs={{0,8},{8,16},{16,24},{24,28},{28,20},{20,12},{12,4},{4,0},{2,6},{1... | collective-permute-start | bytes 1572872 | tf_op jit(solution)/shard_map/ppermute | solution.py:333
  5.2 5.2 %collective-permute-done.1.refs_2_ = bf16[64,4096]{1,0:T(8,128)(2,1)S(1)} collective-permute-done((bf16[64,4096]{1,0:T(8,128)(2,1)}, bf16[64,4096]{1,0:T(8,128)(2,1)S(1)}, u32[]{:S(2)}, u32[]{:S(2)}) %collective-permute-start.1) | collective-permute-done | bytes 524320 | tf_op jit(solution)/shard_map/ppermute | solution.py:333
  10.4 2.1 %collective-permute-start.5 = (bf16[64,4096]{1,0:T(8,128)(2,1)S(1)}, bf16[64,4096]{1,0:T(8,128)(2,1)S(1)}, u32[]{:S(2)}, u32[]{:S(2)}) collective-permute-start(bf16[64,4096]{1,0:T(8,128)(2,1)S(1)} %collective-permute-done.1.refs_2_), channel_id=1, source_target_pairs={{0,8},{8,16},{16,24},{24,28},{28,20},{20,12},{12,4},{4,0},{2,6},{1... | collective-permute-start | bytes 1572872 | tf_op jit(solution)/shard_map/ppermute | solution.py:333
  12.5 3.5 %collective-permute-done.3.refs_0_ = bf16[64,4096]{1,0:T(8,128)(2,1)S(1)} collective-permute-done((bf16[64,4096]{1,0:T(8,128)(2,1)S(1)}, bf16[64,4096]{1,0:T(8,128)(2,1)S(1)}, u32[]{:S(2)}, u32[]{:S(2)}) %collective-permute-start.3) | collective-permute-done | bytes 524320 | tf_op jit(solution)/shard_map/ppermute | solution.py:333
  16.0 2.1 %collective-permute-start.7 = (bf16[64,4096]{1,0:T(8,128)(2,1)S(1)}, bf16[64,4096]{1,0:T(8,128)(2,1)S(1)}, u32[]{:S(2)}, u32[]{:S(2)}) collective-permute-start(bf16[64,4096]{1,0:T(8,128)(2,1)S(1)} %collective-permute-done.3.refs_0_), channel_id=1, source_target_pairs={{0,8},{8,16},{16,24},{24,28},{28,20},{20,12},{12,4},{4,0},{2,6},{1... | collective-permute-start | bytes 1572872 | tf_op jit(solution)/shard_map/ppermute | solution.py:333
  18.1 3.5 %collective-permute-done.5.refs_2_ = bf16[64,4096]{1,0:T(8,128)(2,1)S(1)} collective-permute-done((bf16[64,4096]{1,0:T(8,128)(2,1)S(1)}, bf16[64,4096]{1,0:T(8,128)(2,1)S(1)}, u32[]{:S(2)}, u32[]{:S(2)}) %collective-permute-start.5) | collective-permute-done | bytes 524320 | tf_op jit(solution)/shard_map/ppermute | solution.py:333
  21.6 2.1 %collective-permute-start.9 = (bf16[64,4096]{1,0:T(8,128)(2,1)S(1)}, bf16[64,4096]{1,0:T(8,128)(2,1)S(1)}, u32[]{:S(2)}, u32[]{:S(2)}) collective-permute-start(bf16[64,4096]{1,0:T(8,128)(2,1)S(1)} %collective-permute-done.5.refs_2_), channel_id=1, source_target_pairs={{0,8},{8,16},{16,24},{24,28},{28,20},{20,12},{12,4},{4,0},{2,6},{1... | collective-permute-start | bytes 1572872 | tf_op jit(solution)/shard_map/ppermute | solution.py:333
  23.7 0.0 collective-permute-start.2
  23.7 0.5 collective-permute-start.6
  24.2 3.0 %collective-permute-done.7.refs_0_ = bf16[64,4096]{1,0:T(8,128)(2,1)S(1)} collective-permute-done((bf16[64,4096]{1,0:T(8,128)(2,1)S(1)}, bf16[64,4096]{1,0:T(8,128)(2,1)S(1)}, u32[]{:S(2)}, u32[]{:S(2)}) %collective-permute-start.7) | collective-permute-done | bytes 524320 | tf_op jit(solution)/shard_map/ppermute | solution.py:333
  27.3 2.1 %collective-permute-start.11 = (bf16[64,4096]{1,0:T(8,128)(2,1)S(1)}, bf16[64,4096]{1,0:T(8,128)(2,1)S(1)}, u32[]{:S(2)}, u32[]{:S(2)}) collective-permute-start(bf16[64,4096]{1,0:T(8,128)(2,1)S(1)} %collective-permute-done.7.refs_0_), channel_id=1, source_target_pairs={{0,8},{8,16},{16,24},{24,28},{28,20},{20,12},{12,4},{4,0},{2,6},{1... | collective-permute-start | bytes 1572872 | tf_op jit(solution)/shard_map/ppermute | solution.py:333
  29.4 3.5 %collective-permute-done.9.refs_0_ = bf16[64,4096]{1,0:T(8,128)(2,1)S(1)} collective-permute-done((bf16[64,4096]{1,0:T(8,128)(2,1)S(1)}, bf16[64,4096]{1,0:T(8,128)(2,1)S(1)}, u32[]{:S(2)}, u32[]{:S(2)}) %collective-permute-start.9) | collective-permute-done | bytes 524320 | tf_op jit(solution)/shard_map/ppermute | solution.py:333
  32.9 2.1 %collective-permute-start.13 = (bf16[64,4096]{1,0:T(8,128)(2,1)S(1)}, bf16[64,4096]{1,0:T(8,128)(2,1)S(1)}, u32[]{:S(2)}, u32[]{:S(2)}) collective-permute-start(bf16[64,4096]{1,0:T(8,128)(2,1)S(1)} %collective-permute-done.9.refs_0_), channel_id=1, source_target_pairs={{0,8},{8,16},{16,24},{24,28},{28,20},{20,12},{12,4},{4,0},{2,6},{1... | collective-permute-start | bytes 1572872 | tf_op jit(solution)/shard_map/ppermute | solution.py:333
  35.0 0.0 collective-permute-start.4
  35.0 0.0 collective-permute-done.2.refs_3_
  35.0 0.5 collective-permute-start.8
  35.5 0.0 collective-permute-done.6.refs_3_
  35.5 0.1 collective-permute-start.10
  35.6 4.7 %shard_map.37 = (bf16[1024,4096]{1,0:T(8,128)(2,1)S(1)}, f32[1024,1]{1,0:T(8,128)S(1)}) custom-call(bf16[1024,4096]{1,0:T(8,128)(2,1)} %grad_ref.1), custom_call_target="tpu_custom_call" | custom-call | flops 8388608 | bytes 8388608 | tf_op jit(solution)/shard_map/pallas_call | solution.py:193
  40.2 0.0 collective-permute-done.11.refs_0_
  40.2 0.5 collective-permute-start.12
  40.8 3.4 %collective-permute-done.13.refs_0_ = bf16[64,4096]{1,0:T(8,128)(2,1)S(1)} collective-permute-done((bf16[64,4096]{1,0:T(8,128)(2,1)S(1)}, bf16[64,4096]{1,0:T(8,128)(2,1)S(1)}, u32[]{:S(2)}, u32[]{:S(2)}) %collective-permute-start.13) | collective-permute-done | bytes 524320 | tf_op jit(solution)/shard_map/ppermute | solution.py:333
  44.1 0.0 collective-permute-start.14
  44.1 0.0 copy-done
  44.1 2.5 %shard_map.38 = (bf16[2,1024,128]{2,1,0:T(8,128)(2,1)S(1)}, bf16[1024,4096]{1,0:T(8,128)(2,1)S(1)}) custom-call(bf16[1024,4096]{1,0:T(8,128)(2,1)S(1)} %get-tuple-element.27.grad_ref, bf16[64,4096]{1,0:T(8,128)(2,1)S(1)} %copy-done, bf16[64,4096]{1,0:T(8,128)(2,1)S(1)} %collective-permute-done.refs_1_, ...), custom_call_target="tpu_custom_call", output_to_operand_aliasing={{1}: (0, {})} | custom-call | flops 2147483648 | bytes 8388608 | tf_op jit(solution)/shard_map/pallas_call | solution.py:153
  46.6 0.0 collective-permute-done.4.refs_1_
  46.6 2.5 %shard_map.39 = (bf16[2,1024,128]{2,1,0:T(8,128)(2,1)S(1)}, bf16[1024,4096]{1,0:T(8,128)(2,1)S(1)}) custom-call(bf16[1024,4096]{1,0:T(8,128)(2,1)S(1)} %get-tuple-element.28.grad_ref, bf16[64,4096]{1,0:T(8,128)(2,1)S(1)} %collective-permute-done.3.refs_0_, bf16[64,4096]{1,0:T(8,128)(2,1)S(1)} %collective-permute-done.4.refs_1_, ...), custom_call_target="tpu_custom_call", output_to_operand_aliasing={{1}: (0, {})} | custom-call | flops 2147483648 | bytes 8388608 | tf_op jit(solution)/shard_map/pallas_call | solution.py:153
  49.1 0.0 collective-permute-done.8.refs_1_
  49.1 2.5 %shard_map.40 = (bf16[1,1024,128]{2,1,0:T(8,128)(2,1)S(1)}, bf16[1024,4096]{1,0:T(8,128)(2,1)S(1)}, bf16[1024,128]{1,0:T(8,128)(2,1)S(1)}) custom-call(bf16[1024,4096]{1,0:T(8,128)(2,1)S(1)} %get-tuple-element.29.grad_ref, bf16[64,4096]{1,0:T(8,128)(2,1)S(1)} %collective-permute-done.7.refs_0_, ...), custom_call_target="tpu_custom_call", output_to_operand_aliasing={{1}: (0, {})} | custom-call | flops 1073741824 | bytes 8388608 | tf_op jit(solution)/shard_map/pallas_call | solution.py:153
  51.7 0.0 collective-permute-done.10.refs_1_
  51.7 2.5 %shard_map.41 = (bf16[1,1024,128]{2,1,0:T(8,128)(2,1)S(1)}, bf16[1024,4096]{1,0:T(8,128)(2,1)S(1)}, bf16[1024,128]{1,0:T(8,128)(2,1)S(1)}) custom-call(bf16[1024,4096]{1,0:T(8,128)(2,1)S(1)} %get-tuple-element.32.grad_ref, bf16[64,4096]{1,0:T(8,128)(2,1)S(1)} %collective-permute-done.9.refs_0_, ...), custom_call_target="tpu_custom_call", output_to_operand_aliasing={{1}: (0, {})} | custom-call | flops 1073741824 | bytes 8388608 | tf_op jit(solution)/shard_map/pallas_call | solution.py:153
  54.2 2.1 %collective-permute-start.17 = (bf16[1024,128]{1,0:T(8,128)(2,1)S(1)}, bf16[1024,128]{1,0:T(8,128)(2,1)S(1)}, u32[]{:S(2)}, u32[]{:S(2)}) collective-permute-start(bf16[1024,128]{1,0:T(8,128)(2,1)S(1)} %get-tuple-element.40), channel_id=1, source_target_pairs={{0,1},{1,0},{2,3},{3,2},{4,5},{5,4},{6,7},{7,6},{8,9},{9,8},{10,11... | collective-permute-start | bytes 786440 | tf_op jit(solution)/shard_map/ppermute | solution.py:329
  56.3 0.1 collective-permute-start.16
  56.3 0.0 collective-permute-done.12.refs_1_
  56.3 2.7 %shard_map.42 = (bf16[1,1024,128]{2,1,0:T(8,128)(2,1)S(1)}, bf16[1024,4096]{1,0:T(8,128)(2,1)S(1)}, bf16[1024,128]{1,0:T(8,128)(2,1)S(1)}) custom-call(bf16[1024,4096]{1,0:T(8,128)(2,1)S(1)} %get-tuple-element.34.grad_ref, bf16[64,4096]{1,0:T(8,128)(2,1)S(1)} %collective-permute-done.11.refs_0_, ...), custom_call_target="tpu_custom_call", output_to_operand_aliasing={{1}: (0, {})} | custom-call | flops 1073741824 | bytes 8388608 | tf_op jit(solution)/shard_map/pallas_call | solution.py:153
  59.1 0.0 copy-start.1
  59.1 2.0 %collective-permute-start.18 = (bf16[1024,128]{1,0:T(8,128)(2,1)S(1)}, bf16[1024,128]{1,0:T(8,128)(2,1)S(1)}, u32[]{:S(2)}, u32[]{:S(2)}) collective-permute-start(bf16[1024,128]{1,0:T(8,128)(2,1)S(1)} %get-tuple-element.41), channel_id=1, source_target_pairs={{0,1},{1,0},{2,3},{3,2},{4,5},{5,4},{6,7},{7,6},{8,9},{9,8},{10,11... | collective-permute-start | bytes 786440 | tf_op jit(solution)/shard_map/ppermute | solution.py:329
  61.1 0.0 collective-permute-done.14.refs_1_
  61.1 2.5 %shard_map.43 = (bf16[1,1024,128]{2,1,0:T(8,128)(2,1)S(1)}, bf16[1024,4096]{1,0:T(8,128)(2,1)S(1)}, bf16[1024,128]{1,0:T(8,128)(2,1)S(1)}) custom-call(bf16[1024,4096]{1,0:T(8,128)(2,1)S(1)} %get-tuple-element.36.grad_ref, bf16[64,4096]{1,0:T(8,128)(2,1)S(1)} %collective-permute-done.13.refs_0_, ...), custom_call_target="tpu_custom_call", output_to_operand_aliasing={{1}: (0, {})} | custom-call | flops 1073741824 | bytes 8388608 | tf_op jit(solution)/shard_map/pallas_call | solution.py:153
  63.6 0.1 collective-permute-start.15
  63.7 1.9 %collective-permute-start.19 = (f32[1024,1]{1,0:T(8,128)S(1)}, f32[1024,1]{1,0:T(8,128)S(1)}, u32[]{:S(2)}, u32[]{:S(2)}) collective-permute-start(f32[1024,1]{1,0:T(8,128)S(1)} %get-tuple-element.42.refs_3_), channel_id=1, source_target_pairs={{0,1},{1,0},{2,3},{3,2},{4,5},{5,4},{6,7},{7,6},{8,9},{9,8},{10,11... | collective-permute-start | bytes 12296 | tf_op jit(solution)/shard_map/ppermute | solution.py:329
  65.7 25.6 %collective-permute-done.19.refs_4_ = f32[1024,1]{1,0:T(8,128)S(1)} collective-permute-done((f32[1024,1]{1,0:T(8,128)S(1)}, f32[1024,1]{1,0:T(8,128)S(1)}, u32[]{:S(2)}, u32[]{:S(2)}) %collective-permute-start.19) | collective-permute-done | bytes 4128 | tf_op jit(solution)/shard_map/ppermute | solution.py:329
  91.3 0.0 collective-permute-done.17.refs_1_
  91.3 0.0 collective-permute-done.16.refs_0_
  91.3 0.0 collective-permute-done.18.refs_2_
  91.3 0.0 copy-done.1
  91.3 1.5 %shard_map.44 = (f32[3,1024,128]{2,1,0:T(8,128)S(1)}, f32[3,2,128]{2,1,0:T(2,128)S(1)}, f32[1024,1]{1,0:T(8,128)S(1)}) custom-call(bf16[1024,128]{1,0:T(8,128)(2,1)S(1)} %collective-permute-done.16.refs_0_, bf16[1024,128]{1,0:T(8,128)(2,1)S(1)} %collective-permute-done.17.refs_1_, bf16[1024,128]{1,0:T(8,128)(2,1)S(1)} %collective-permute-done.18.refs_2_, ...), custom_call_target="tpu_custom_call" | custom-call | flops 3145728 | bytes 4718592 | tf_op jit(solution)/shard_map/pallas_call | solution.py:262
  92.9 0.0 collective-permute-done.15.refs_0_
  92.9 0.5 shard_map.45
  93.4 0.1 collective-permute-start.20
  93.4 1.2 %collective-permute-done.20 = f32[2,512]{1,0:T(2,128)S(1)} collective-permute-done((f32[2,512]{1,0:T(2,128)S(1)}, f32[2,512]{1,0:T(2,128)S(1)}, u32[]{:S(2)}, u32[]{:S(2)}) %collective-permute-start.20) | collective-permute-done | bytes 4128 | tf_op jit(solution)/shard_map/ppermute | solution.py:359
  94.6 1.8 %collective-permute-start.21 = (f32[2,512]{1,0:T(2,128)S(1)}, f32[2,512]{1,0:T(2,128)S(1)}, u32[]{:S(2)}, u32[]{:S(2)}) collective-permute-start(f32[2,512]{1,0:T(2,128)S(1)} %pad_maximum_fusion), channel_id=1, source_target_pairs={{0,4},{2,6},{4,0},{6,2},{8,12},{10,14},{12,8},{14,10},{16,20},{18,... | collective-permute-start | bytes 12296 | tf_op jit(solution)/shard_map/ppermute | solution.py:359
  96.4 1.9 %collective-permute-done.21 = f32[2,512]{1,0:T(2,128)S(1)} collective-permute-done((f32[2,512]{1,0:T(2,128)S(1)}, f32[2,512]{1,0:T(2,128)S(1)}, u32[]{:S(2)}, u32[]{:S(2)}) %collective-permute-start.21) | collective-permute-done | bytes 4128 | tf_op jit(solution)/shard_map/ppermute | solution.py:359
  98.3 1.9 %collective-permute-start.22 = (f32[2,512]{1,0:T(2,128)S(1)}, f32[2,512]{1,0:T(2,128)S(1)}, u32[]{:S(2)}, u32[]{:S(2)}) collective-permute-start(f32[2,512]{1,0:T(2,128)S(1)} %pad_maximum_fusion.1), channel_id=1, source_target_pairs={{0,8},{2,10},{4,12},{6,14},{8,0},{10,2},{12,4},{14,6},{16,24},{18,... | collective-permute-start | bytes 12296 | tf_op jit(solution)/shard_map/ppermute | solution.py:359
  100.2 1.8 %collective-permute-done.22 = f32[2,512]{1,0:T(2,128)S(1)} collective-permute-done((f32[2,512]{1,0:T(2,128)S(1)}, f32[2,512]{1,0:T(2,128)S(1)}, u32[]{:S(2)}, u32[]{:S(2)}) %collective-permute-start.22) | collective-permute-done | bytes 4128 | tf_op jit(solution)/shard_map/ppermute | solution.py:359
  102.0 2.9 %collective-permute-start.23 = (f32[2,512]{1,0:T(2,128)S(1)}, f32[2,512]{1,0:T(2,128)S(1)}, u32[]{:S(2)}, u32[]{:S(2)}) collective-permute-start(f32[2,512]{1,0:T(2,128)S(1)} %pad_maximum_fusion.2), channel_id=1, source_target_pairs={{0,16},{2,18},{4,20},{6,22},{8,24},{10,26},{12,28},{14,30},{16,0},... | collective-permute-start | bytes 12296 | tf_op jit(solution)/shard_map/ppermute | solution.py:359
  104.9 1.7 %collective-permute-done.23 = f32[2,512]{1,0:T(2,128)S(1)} collective-permute-done((f32[2,512]{1,0:T(2,128)S(1)}, f32[2,512]{1,0:T(2,128)S(1)}, u32[]{:S(2)}, u32[]{:S(2)}) %collective-permute-start.23) | collective-permute-done | bytes 4128 | tf_op jit(solution)/shard_map/ppermute | solution.py:359
  106.6 1.4 %shard_map.46 = bf16[1024,512]{1,0:T(8,128)(2,1)} custom-call(f32[2,512]{1,0:T(2,128)S(1)} %pad_maximum_fusion.3.stat_ref, f32[3,1024,128]{2,1,0:T(8,128)S(1)} %get-tuple-element.47.early_ref, f32[1,1024,128]{2,1,0:T(8,128)S(1)} %get-tuple-element.48.late_ref), custom_call_target="tpu_custom_call" | custom-call | flops 1048576 | bytes 3145728 | tf_op jit(solution)/shard_map/pallas_call | solution.py:292
  (8 shorter events, 0.1 us)
Async XLA Ops:
  0.0 44.1 %copy-start = (bf16[64,4096]{1,0:T(8,128)(2,1)S(1)}, bf16[64,4096]{1,0:T(8,128)(2,1)}, u32[]{:S(2)}) copy-start(bf16[64,4096]{1,0:T(8,128)(2,1)} %refs_0_.1) | copy-start | bytes 1572868
  0.0 3.1 %collective-permute-start = (bf16[64,4096]{1,0:T(8,128)(2,1)}, bf16[64,4096]{1,0:T(8,128)(2,1)S(1)}, u32[]{:S(2)}, u32[]{:S(2)}) collective-permute-start(bf16[64,4096]{1,0:T(8,128)(2,1)} %refs_0_.1), channel_id=1, source_target_pairs={{0,2},{2,0},{4,6},{6,4},{8,10},{10,8},{12,14},{14,12},{16,18},{18,... | collective-permute-start | bytes 1572872 | tf_op jit(solution)/shard_map/ppermute | solution.py:331
  0.5 9.9 %collective-permute-start.1 = (bf16[64,4096]{1,0:T(8,128)(2,1)}, bf16[64,4096]{1,0:T(8,128)(2,1)S(1)}, u32[]{:S(2)}, u32[]{:S(2)}) collective-permute-start(bf16[64,4096]{1,0:T(8,128)(2,1)} %refs_0_.1), channel_id=1, source_target_pairs={{0,8},{8,16},{16,24},{24,28},{28,20},{20,12},{12,4},{4,0},{2,6},{1... | collective-permute-start | bytes 1572872 | tf_op jit(solution)/shard_map/ppermute | solution.py:333
  3.1 12.9 %collective-permute-start.3 = (bf16[64,4096]{1,0:T(8,128)(2,1)S(1)}, bf16[64,4096]{1,0:T(8,128)(2,1)S(1)}, u32[]{:S(2)}, u32[]{:S(2)}) collective-permute-start(bf16[64,4096]{1,0:T(8,128)(2,1)S(1)} %collective-permute-done.refs_1_), channel_id=1, source_target_pairs={{0,8},{8,16},{16,24},{24,28},{28,20},{20,12},{12,4},{4,0},{2,6},{1... | collective-permute-start | bytes 1572872 | tf_op jit(solution)/shard_map/ppermute | solution.py:333
  10.4 11.2 %collective-permute-start.5 = (bf16[64,4096]{1,0:T(8,128)(2,1)S(1)}, bf16[64,4096]{1,0:T(8,128)(2,1)S(1)}, u32[]{:S(2)}, u32[]{:S(2)}) collective-permute-start(bf16[64,4096]{1,0:T(8,128)(2,1)S(1)} %collective-permute-done.1.refs_2_), channel_id=1, source_target_pairs={{0,8},{8,16},{16,24},{24,28},{28,20},{20,12},{12,4},{4,0},{2,6},{1... | collective-permute-start | bytes 1572872 | tf_op jit(solution)/shard_map/ppermute | solution.py:333
  16.0 11.2 %collective-permute-start.7 = (bf16[64,4096]{1,0:T(8,128)(2,1)S(1)}, bf16[64,4096]{1,0:T(8,128)(2,1)S(1)}, u32[]{:S(2)}, u32[]{:S(2)}) collective-permute-start(bf16[64,4096]{1,0:T(8,128)(2,1)S(1)} %collective-permute-done.3.refs_0_), channel_id=1, source_target_pairs={{0,8},{8,16},{16,24},{24,28},{28,20},{20,12},{12,4},{4,0},{2,6},{1... | collective-permute-start | bytes 1572872 | tf_op jit(solution)/shard_map/ppermute | solution.py:333
  21.6 11.2 %collective-permute-start.9 = (bf16[64,4096]{1,0:T(8,128)(2,1)S(1)}, bf16[64,4096]{1,0:T(8,128)(2,1)S(1)}, u32[]{:S(2)}, u32[]{:S(2)}) collective-permute-start(bf16[64,4096]{1,0:T(8,128)(2,1)S(1)} %collective-permute-done.5.refs_2_), channel_id=1, source_target_pairs={{0,8},{8,16},{16,24},{24,28},{28,20},{20,12},{12,4},{4,0},{2,6},{1... | collective-permute-start | bytes 1572872 | tf_op jit(solution)/shard_map/ppermute | solution.py:333
  23.7 11.2 %collective-permute-start.2 = (bf16[64,4096]{1,0:T(8,128)(2,1)S(1)}, bf16[64,4096]{1,0:T(8,128)(2,1)S(1)}, u32[]{:S(2)}, u32[]{:S(2)}) collective-permute-start(bf16[64,4096]{1,0:T(8,128)(2,1)S(1)} %collective-permute-done.1.refs_2_), channel_id=1, source_target_pairs={{0,2},{2,0},{4,6},{6,4},{8,10},{10,8},{12,14},{14,12},{16,18},{18,... | collective-permute-start | bytes 1572872 | tf_op jit(solution)/shard_map/ppermute | solution.py:336
  23.7 11.8 %collective-permute-start.6 = (bf16[64,4096]{1,0:T(8,128)(2,1)S(1)}, bf16[64,4096]{1,0:T(8,128)(2,1)S(1)}, u32[]{:S(2)}, u32[]{:S(2)}) collective-permute-start(bf16[64,4096]{1,0:T(8,128)(2,1)S(1)} %collective-permute-done.5.refs_2_), channel_id=1, source_target_pairs={{0,2},{2,0},{4,6},{6,4},{8,10},{10,8},{12,14},{14,12},{16,18},{18,... | collective-permute-start | bytes 1572872 | tf_op jit(solution)/shard_map/ppermute | solution.py:336
  27.3 13.0 %collective-permute-start.11 = (bf16[64,4096]{1,0:T(8,128)(2,1)S(1)}, bf16[64,4096]{1,0:T(8,128)(2,1)S(1)}, u32[]{:S(2)}, u32[]{:S(2)}) collective-permute-start(bf16[64,4096]{1,0:T(8,128)(2,1)S(1)} %collective-permute-done.7.refs_0_), channel_id=1, source_target_pairs={{0,8},{8,16},{16,24},{24,28},{28,20},{20,12},{12,4},{4,0},{2,6},{1... | collective-permute-start | bytes 1572872 | tf_op jit(solution)/shard_map/ppermute | solution.py:333
  32.9 11.2 %collective-permute-start.13 = (bf16[64,4096]{1,0:T(8,128)(2,1)S(1)}, bf16[64,4096]{1,0:T(8,128)(2,1)S(1)}, u32[]{:S(2)}, u32[]{:S(2)}) collective-permute-start(bf16[64,4096]{1,0:T(8,128)(2,1)S(1)} %collective-permute-done.9.refs_0_), channel_id=1, source_target_pairs={{0,8},{8,16},{16,24},{24,28},{28,20},{20,12},{12,4},{4,0},{2,6},{1... | collective-permute-start | bytes 1572872 | tf_op jit(solution)/shard_map/ppermute | solution.py:333
  35.0 11.6 %collective-permute-start.4 = (bf16[64,4096]{1,0:T(8,128)(2,1)S(1)}, bf16[64,4096]{1,0:T(8,128)(2,1)S(1)}, u32[]{:S(2)}, u32[]{:S(2)}) collective-permute-start(bf16[64,4096]{1,0:T(8,128)(2,1)S(1)} %collective-permute-done.3.refs_0_), channel_id=1, source_target_pairs={{0,2},{2,0},{4,6},{6,4},{8,10},{10,8},{12,14},{14,12},{16,18},{18,... | collective-permute-start | bytes 1572872 | tf_op jit(solution)/shard_map/ppermute | solution.py:336
  35.0 14.1 %collective-permute-start.8 = (bf16[64,4096]{1,0:T(8,128)(2,1)S(1)}, bf16[64,4096]{1,0:T(8,128)(2,1)S(1)}, u32[]{:S(2)}, u32[]{:S(2)}) collective-permute-start(bf16[64,4096]{1,0:T(8,128)(2,1)S(1)} %collective-permute-done.7.refs_0_), channel_id=1, source_target_pairs={{0,2},{2,0},{4,6},{6,4},{8,10},{10,8},{12,14},{14,12},{16,18},{18,... | collective-permute-start | bytes 1572872 | tf_op jit(solution)/shard_map/ppermute | solution.py:336
  35.5 16.2 %collective-permute-start.10 = (bf16[64,4096]{1,0:T(8,128)(2,1)S(1)}, bf16[64,4096]{1,0:T(8,128)(2,1)S(1)}, u32[]{:S(2)}, u32[]{:S(2)}) collective-permute-start(bf16[64,4096]{1,0:T(8,128)(2,1)S(1)} %collective-permute-done.9.refs_0_), channel_id=1, source_target_pairs={{0,2},{2,0},{4,6},{6,4},{8,10},{10,8},{12,14},{14,12},{16,18},{18,... | collective-permute-start | bytes 1572872 | tf_op jit(solution)/shard_map/ppermute | solution.py:336
  40.2 16.1 %collective-permute-start.12 = (bf16[64,4096]{1,0:T(8,128)(2,1)S(1)}, bf16[64,4096]{1,0:T(8,128)(2,1)S(1)}, u32[]{:S(2)}, u32[]{:S(2)}) collective-permute-start(bf16[64,4096]{1,0:T(8,128)(2,1)S(1)} %collective-permute-done.11.refs_0_), channel_id=1, source_target_pairs={{0,2},{2,0},{4,6},{6,4},{8,10},{10,8},{12,14},{14,12},{16,18},{18,... | collective-permute-start | bytes 1572872 | tf_op jit(solution)/shard_map/ppermute | solution.py:336
  44.1 17.0 %collective-permute-start.14 = (bf16[64,4096]{1,0:T(8,128)(2,1)S(1)}, bf16[64,4096]{1,0:T(8,128)(2,1)S(1)}, u32[]{:S(2)}, u32[]{:S(2)}) collective-permute-start(bf16[64,4096]{1,0:T(8,128)(2,1)S(1)} %collective-permute-done.13.refs_0_), channel_id=1, source_target_pairs={{0,2},{2,0},{4,6},{6,4},{8,10},{10,8},{12,14},{14,12},{16,18},{18,... | collective-permute-start | bytes 1572872 | tf_op jit(solution)/shard_map/ppermute | solution.py:336
  54.2 37.1 %collective-permute-start.17 = (bf16[1024,128]{1,0:T(8,128)(2,1)S(1)}, bf16[1024,128]{1,0:T(8,128)(2,1)S(1)}, u32[]{:S(2)}, u32[]{:S(2)}) collective-permute-start(bf16[1024,128]{1,0:T(8,128)(2,1)S(1)} %get-tuple-element.40), channel_id=1, source_target_pairs={{0,1},{1,0},{2,3},{3,2},{4,5},{5,4},{6,7},{7,6},{8,9},{9,8},{10,11... | collective-permute-start | bytes 786440 | tf_op jit(solution)/shard_map/ppermute | solution.py:329
  56.3 35.1 %collective-permute-start.16 = (bf16[1024,128]{1,0:T(8,128)(2,1)S(1)}, bf16[1024,128]{1,0:T(8,128)(2,1)S(1)}, u32[]{:S(2)}, u32[]{:S(2)}) collective-permute-start(bf16[1024,128]{1,0:T(8,128)(2,1)S(1)} %get-tuple-element.39), channel_id=1, source_target_pairs={{0,1},{1,0},{2,3},{3,2},{4,5},{5,4},{6,7},{7,6},{8,9},{9,8},{10,11... | collective-permute-start | bytes 786440 | tf_op jit(solution)/shard_map/ppermute | solution.py:329
  59.1 32.3 %copy-start.1 = (f32[1024]{0:T(1024)S(1)}, f32[1024]{0:T(1024)}, u32[]{:S(2)}) copy-start(f32[1024]{0:T(1024)} %param.5) | copy-start | bytes 12292
  59.1 32.3 %collective-permute-start.18 = (bf16[1024,128]{1,0:T(8,128)(2,1)S(1)}, bf16[1024,128]{1,0:T(8,128)(2,1)S(1)}, u32[]{:S(2)}, u32[]{:S(2)}) collective-permute-start(bf16[1024,128]{1,0:T(8,128)(2,1)S(1)} %get-tuple-element.41), channel_id=1, source_target_pairs={{0,1},{1,0},{2,3},{3,2},{4,5},{5,4},{6,7},{7,6},{8,9},{9,8},{10,11... | collective-permute-start | bytes 786440 | tf_op jit(solution)/shard_map/ppermute | solution.py:329
  63.6 29.3 %collective-permute-start.15 = (bf16[1024,128]{1,0:T(8,128)(2,1)S(1)}, bf16[1024,128]{1,0:T(8,128)(2,1)S(1)}, u32[]{:S(2)}, u32[]{:S(2)}) collective-permute-start(bf16[1024,128]{1,0:T(8,128)(2,1)S(1)} %get-tuple-element.38), channel_id=1, source_target_pairs={{0,1},{1,0},{2,3},{3,2},{4,5},{5,4},{6,7},{7,6},{8,9},{9,8},{10,11... | collective-permute-start | bytes 786440 | tf_op jit(solution)/shard_map/ppermute | solution.py:329
  63.7 27.6 %collective-permute-start.19 = (f32[1024,1]{1,0:T(8,128)S(1)}, f32[1024,1]{1,0:T(8,128)S(1)}, u32[]{:S(2)}, u32[]{:S(2)}) collective-permute-start(f32[1024,1]{1,0:T(8,128)S(1)} %get-tuple-element.42.refs_3_), channel_id=1, source_target_pairs={{0,1},{1,0},{2,3},{3,2},{4,5},{5,4},{6,7},{7,6},{8,9},{9,8},{10,11... | collective-permute-start | bytes 12296 | tf_op jit(solution)/shard_map/ppermute | solution.py:329
  93.4 1.2 %collective-permute-start.20 = (f32[2,512]{1,0:T(2,128)S(1)}, f32[2,512]{1,0:T(2,128)S(1)}, u32[]{:S(2)}, u32[]{:S(2)}) collective-permute-start(f32[2,512]{1,0:T(2,128)S(1)} %get-tuple-element.46), channel_id=1, source_target_pairs={{0,2},{2,0},{4,6},{6,4},{8,10},{10,8},{12,14},{14,12},{16,18},{18,... | collective-permute-start | bytes 12296 | tf_op jit(solution)/shard_map/ppermute | solution.py:359
  94.6 3.7 %collective-permute-start.21 = (f32[2,512]{1,0:T(2,128)S(1)}, f32[2,512]{1,0:T(2,128)S(1)}, u32[]{:S(2)}, u32[]{:S(2)}) collective-permute-start(f32[2,512]{1,0:T(2,128)S(1)} %pad_maximum_fusion), channel_id=1, source_target_pairs={{0,4},{2,6},{4,0},{6,2},{8,12},{10,14},{12,8},{14,10},{16,20},{18,... | collective-permute-start | bytes 12296 | tf_op jit(solution)/shard_map/ppermute | solution.py:359
  98.3 3.7 %collective-permute-start.22 = (f32[2,512]{1,0:T(2,128)S(1)}, f32[2,512]{1,0:T(2,128)S(1)}, u32[]{:S(2)}, u32[]{:S(2)}) collective-permute-start(f32[2,512]{1,0:T(2,128)S(1)} %pad_maximum_fusion.1), channel_id=1, source_target_pairs={{0,8},{2,10},{4,12},{6,14},{8,0},{10,2},{12,4},{14,6},{16,24},{18,... | collective-permute-start | bytes 12296 | tf_op jit(solution)/shard_map/ppermute | solution.py:359
  102.0 4.6 %collective-permute-start.23 = (f32[2,512]{1,0:T(2,128)S(1)}, f32[2,512]{1,0:T(2,128)S(1)}, u32[]{:S(2)}, u32[]{:S(2)}) collective-permute-start(f32[2,512]{1,0:T(2,128)S(1)} %pad_maximum_fusion.2), channel_id=1, source_target_pairs={{0,16},{2,18},{4,20},{6,22},{8,24},{10,26},{12,28},{14,30},{16,0},... | collective-permute-start | bytes 12296 | tf_op jit(solution)/shard_map/ppermute | solution.py:359
where the time goes:
time: 108 us
  waiting for transfers between devices  54.3 us (50%)
  starting transfers between devices  30.1 us (28%)
  Pallas kernels  23.3 us (22%)
    ppermute x5, waiting for transfers between devices, cross(): return lax.ppermute(value, 'feat', [(0, 1), (1, 0)])  25.7 us
    ppermute x7, waiting for transfers between devices, ring_body(): ring.append(lax.ppermute(ring[-2], 'rows', turn))  22.2 us
    pallas_call x6, Pallas kernels, product_call(): pl.pallas_call(functools.partial(product_kernel, plan, sources, count, tu...  15.2 us
    ppermute x7, starting transfers between devices, ring_body(): ring.append(lax.ppermute(ring[-2], 'rows', turn))  15.1 us
    ppermute x4, starting transfers between devices, ring_body(): come = lax.ppermute(jnp.concatenate([mean, spread], axis=0), 'rows', pairs)  6.68 us
    ppermute x4, waiting for transfers between devices, ring_body(): come = lax.ppermute(jnp.concatenate([mean, spread], axis=0), 'rows', pairs)  6.46 us
    ppermute x5, starting transfers between devices, cross(): return lax.ppermute(value, 'feat', [(0, 1), (1, 0)])  6.25 us
    pallas_call x1, Pallas kernels, load_call(): pl.pallas_call(functools.partial(load_kernel, parts), out_shape=[jax.Shap...  4.67 us
  transfers between devices with their start and end apart: 24, of which 11 were waited for; matrix products, arithmetic and copies ran while one was open for 0% of the time, Pallas kernels for 20%

commit v1 on v0

--- a/solution.py
+++ b/solution.py
@@ -164,7 +164,11 @@
     )(gradients, *units, *[a for _, a in known])
 
 
-def load_kernel(parts, grad_ref, held_ref, square_ref, sem):
+def diagonal():
+    return lax.broadcasted_iota(jnp.int32, (128, 128), 0) == lax.broadcasted_iota(jnp.int32, (128, 128), 1)
+
+
+def load_kernel(parts, grad_ref, held_ref, square_ref, sums_ref, sem):
     rows, depth = held_ref.shape
     piece = rows // parts
     copies = [
@@ -182,10 +186,13 @@
             for c in range(depth // 128):
                 wide = held_ref[here, c * 128:(c + 1) * 128].astype(jnp.float32)
                 total = total + wide * wide
-            square_ref[here, :] = jnp.sum(total, axis=1, keepdims=True)
+            sums_ref[here, :] = jnp.sum(total, axis=1, keepdims=True)
             return carry
 
         lax.fori_loop(0, piece // 64, step, 0)
+    for i in range(square_ref.shape[0]):
+        column = sums_ref[i * 128:(i + 1) * 128, :]
+        square_ref[i:i + 1, :] = jnp.sum(jnp.where(diagonal(), column, 0.0), axis=0, keepdims=True)
 
 
 def load_call(gradients, parts=4):
@@ -194,11 +201,11 @@
         functools.partial(load_kernel, parts),
         out_shape=[
             jax.ShapeDtypeStruct((rows, depth), gradients.dtype),
-            jax.ShapeDtypeStruct((rows, 1), jnp.float32),
+            jax.ShapeDtypeStruct((rows // 128, 128), jnp.float32),
         ],
         in_specs=[pl.BlockSpec(memory_space=pltpu.HBM)],
         out_specs=[VMEM, VMEM],
-        scratch_shapes=[pltpu.SemaphoreType.DMA((parts,))],
+        scratch_shapes=[pltpu.VMEM((rows, 1), jnp.float32), pltpu.SemaphoreType.DMA((parts,))],
         compiler_params=pltpu.CompilerParams(vmem_limit_bytes=8 * 1024 * 1024),
         cost_estimate=pl.CostEstimate(flops=2 * rows * depth, bytes_accessed=2 * rows * depth, transcendentals=0),
     )(pltpu.with_memory_space_constraint(gradients, pltpu.HBM))
@@ -213,12 +220,10 @@
     older, refs = refs[:len(known)], refs[len(known):]
     if first:
         scored_ref, stat_ref, factor_ref, pick = refs
-        eye = lax.broadcasted_iota(jnp.int32, (128, 128), 0) == lax.broadcasted_iota(jnp.int32, (128, 128), 1)
-        for i in range(weight_ref.shape[0]):
-            rows = slice(i * 128, (i + 1) * 128)
-            weight = jnp.sum(jnp.where(eye, weight_ref[i:i + 1, :], 0.0), axis=1, keepdims=True)
-            squares = square_ref[rows, :] + other_ref[rows, :]
-            factor_ref[rows, :] = weight / jnp.sqrt(squares / depth + NORM_EPS)
+        factor = weight_ref[...] / jnp.sqrt((square_ref[...] + other_ref[...]) / depth + NORM_EPS)
+        for i in range(factor.shape[0]):
+            column = jnp.sum(jnp.where(diagonal(), factor[i:i + 1, :], 0.0), axis=1, keepdims=True)
+            factor_ref[i * 128:(i + 1) * 128, :] = column
     else:
         scored_ref, stat_ref, pick = refs
     blocks = block_readers(known, older)
@@ -270,11 +275,12 @@
     )(*args)
 
 
-def finish_kernel(plan, count, stat_ref, early_ref, late_ref, out_ref):
+def finish_kernel(plan, count, own_ref, back_ref, early_ref, late_ref, out_ref):
     lane = lax.broadcasted_iota(jnp.int32, late_ref.shape[1:], 1)
     codes = [plan.packed(plan.place, half) for half in range(2)]
     early = early_ref.shape[0]
-    scale = lax.rsqrt(stat_ref[1:2, :] / count + VAR_EPS)
+    stat = jnp.where(lax.axis_index("rows") % 2 == 1, own_ref[...], back_ref[...])
+    mean, scale = stat[0:1, :], lax.rsqrt(stat[1:2, :] / count + VAR_EPS)
     for j in range(plan.turns):
         halves = []
         for half in range(2):
@@ -283,27 +289,27 @@
             halves.append(jnp.where(index < early, value, late_ref[0]))
         value = jnp.where(lane < 64, halves[0], halves[1])
         columns = slice(j * 128, (j + 1) * 128)
-        out_ref[:, columns] = ((value - stat_ref[0:1, columns]) * scale[:, columns]).astype(jnp.bfloat16)
-
-
-def finish_call(plan, count, stat, early, late):
+        out_ref[:, columns] = ((value - mean[:, columns]) * scale[:, columns]).astype(jnp.bfloat16)
+
+
+def finish_call(plan, count, own, back, early, late):
     rows = late.shape[1]
     width = plan.turns * 128
     return pl.pallas_call(
         functools.partial(finish_kernel, plan, count),
         out_shape=jax.ShapeDtypeStruct((rows, width), jnp.bfloat16),
-        in_specs=[VMEM] * 3,
+        in_specs=[VMEM] * 4,
         out_specs=VMEM,
         compiler_params=pltpu.CompilerParams(vmem_limit_bytes=8 * 1024 * 1024),
         cost_estimate=pl.CostEstimate(flops=2 * rows * width, bytes_accessed=6 * rows * width, transcendentals=0),
-    )(stat, early, late)
+    )(own, back, early, late)
 
 
 def product_groups(plan):
     groups, p, m = [], 0, 0
     while p < plan.pairs:
         ready = max(max(plan.options(plan.give, half, m)) for half in range(2))
-        n = 2 if p + 1 < ready and p + 1 < plan.pairs else 1
+        n = 2 if p == 0 or p + 1 == ready else 1
         done = p + n > ready
         groups.append((p, n, m if done else None))
         m += done
@@ -352,17 +358,23 @@
     early, stat, factor = score_call(plan, list(range(last)), comes[:last], known, feature_count, squares)
     late, stat = score_call(plan, [last], comes[last:], known, feature_count, None, factor, stat)
 
+    chips = [r for r in range(2 * nodes) if r % 2 == 1]
+    ways = [[(r - 1, r) for r in chips]]
+    step = 2
+    while step < 2 * nodes:
+        ways.append([(r, r ^ step) for r in chips])
+        step *= 2
     mean, spread = stat[0:1], stat[1:2]
-    count, step = rows_here, 1
-    while step < 2 * nodes:
-        pairs = [(r, r ^ step) for r in range(2 * nodes)]
+    count = rows_here
+    for pairs in ways:
         come = lax.ppermute(jnp.concatenate([mean, spread], axis=0), "rows", pairs)
         gap = come[0:1] - mean
         mean = 0.5 * (mean + come[0:1])
         spread = spread + come[1:2] + (0.5 * count) * (gap * gap)
         count *= 2
-        step *= 2
-    return finish_call(plan, count, jnp.concatenate([mean, spread], axis=0), early, late)
+    stat = jnp.concatenate([mean, spread], axis=0)
+    back = lax.ppermute(stat, "rows", [(r, r - 1) for r in chips])
+    return finish_call(plan, count, stat, back, early, late)
 
 
 def solution(mesh):

time: 108 us -> 103 us (0.954)
  waiting for transfers between devices: 54.3 us -> 50.2 us
  starting transfers between devices: 30.1 us -> 28.5 us
    ppermute x0 -> x1, waiting for transfers between devices: none -> 12.9 us  [ring_body(): back = lax.ppermute(stat, 'rows', [(r, r - 1) for r in chips])]
    ppermute x5, waiting for transfers between devices: 25.7 us -> 14.5 us  [cross(): return lax.ppermute(value, 'feat', [(0, 1), (1, 0)])]
    ppermute x4, waiting for transfers between devices: 6.46 us -> 0.81 us  [ring_body(): come = lax.ppermute(jnp.concatenate([mean, spread], axis=0), 'rows', pairs)]
    ppermute x4, starting transfers between devices: 6.68 us -> 3.8 us  [ring_body(): come = lax.ppermute(jnp.concatenate([mean, spread], axis=0), 'rows', pairs)]
    ppermute x0 -> x1, starting transfers between devices: none -> 1.29 us  [ring_body(): back = lax.ppermute(stat, 'rows', [(r, r - 1) for r in chips])]
  transfers between devices with their start and end apart: 24 -> 25, of which waited for: 11 -> 9; matrix products, arithmetic and copies ran while one was open for 0% -> 0% of each run, Pallas kernels for 20% -> 21%
where the time goes in v1:
time: 103 us
  waiting for transfers between devices  50.2 us (49%)
  starting transfers between devices  28.5 us (28%)
  Pallas kernels  23.5 us (23%)
    ppermute x7, waiting for transfers between devices, ring_body(): ring.append(lax.ppermute(ring[-2], 'rows', turn))  22 us
    pallas_call x6, Pallas kernels, product_call(): pl.pallas_call(functools.partial(product_kernel, plan, sources, count, tu...  15.1 us
    ppermute x7, starting transfers between devices, ring_body(): ring.append(lax.ppermute(ring[-2], 'rows', turn))  15.1 us
    ppermute x5, waiting for transfers between devices, cross(): return lax.ppermute(value, 'feat', [(0, 1), (1, 0)])  14.5 us
    ppermute x1, waiting for transfers between devices, ring_body(): back = lax.ppermute(stat, 'rows', [(r, r - 1) for r in chips])  12.9 us
    ppermute x5, starting transfers between devices, cross(): return lax.ppermute(value, 'feat', [(0, 1), (1, 0)])  6.25 us
    pallas_call x1, Pallas kernels, load_call(): pl.pallas_call(functools.partial(load_kernel, parts), out_shape=[jax.Shap...  4.9 us
    ppermute x4, starting transfers between devices, ring_body(): come = lax.ppermute(jnp.concatenate([mean, spread], axis=0), 'rows', pairs)  3.8 us
  transfers between devices with their start and end apart: 25, of which 9 were waited for; matrix products, arithmetic and copies ran while one was open for 0% of the time, Pallas kernels for 21%

profile of v1, /device:TPU:0, one launch (start us, length us, event | category | flops | bytes accessed | tf_op | source)
XLA Modules:
  0.0 102.6 jit_solution(8862783464476609824)
XLA Ops:
  0.0 0.0 copy-start
  0.0 0.5 collective-permute-start
  0.5 2.6 %collective-permute-start.1 = (bf16[64,4096]{1,0:T(8,128)(2,1)}, bf16[64,4096]{1,0:T(8,128)(2,1)S(1)}, u32[]{:S(2)}, u32[]{:S(2)}) collective-permute-start(bf16[64,4096]{1,0:T(8,128)(2,1)} %refs_0_.1), channel_id=1, source_target_pairs={{0,8},{8,16},{16,24},{24,28},{28,20},{20,12},{12,4},{4,0},{2,6},{1... | collective-permute-start | bytes 1572872 | tf_op jit(solution)/shard_map/ppermute | solution.py:339
  3.1 0.0 collective-permute-done.refs_1_
  3.1 2.1 %collective-permute-start.3 = (bf16[64,4096]{1,0:T(8,128)(2,1)S(1)}, bf16[64,4096]{1,0:T(8,128)(2,1)S(1)}, u32[]{:S(2)}, u32[]{:S(2)}) collective-permute-start(bf16[64,4096]{1,0:T(8,128)(2,1)S(1)} %collective-permute-done.refs_1_), channel_id=1, source_target_pairs={{0,8},{8,16},{16,24},{24,28},{28,20},{20,12},{12,4},{4,0},{2,6},{1... | collective-permute-start | bytes 1572872 | tf_op jit(solution)/shard_map/ppermute | solution.py:339
  5.2 5.2 %collective-permute-done.1.refs_2_ = bf16[64,4096]{1,0:T(8,128)(2,1)S(1)} collective-permute-done((bf16[64,4096]{1,0:T(8,128)(2,1)}, bf16[64,4096]{1,0:T(8,128)(2,1)S(1)}, u32[]{:S(2)}, u32[]{:S(2)}) %collective-permute-start.1) | collective-permute-done | bytes 524320 | tf_op jit(solution)/shard_map/ppermute | solution.py:339
  10.4 2.1 %collective-permute-start.5 = (bf16[64,4096]{1,0:T(8,128)(2,1)S(1)}, bf16[64,4096]{1,0:T(8,128)(2,1)S(1)}, u32[]{:S(2)}, u32[]{:S(2)}) collective-permute-start(bf16[64,4096]{1,0:T(8,128)(2,1)S(1)} %collective-permute-done.1.refs_2_), channel_id=1, source_target_pairs={{0,8},{8,16},{16,24},{24,28},{28,20},{20,12},{12,4},{4,0},{2,6},{1... | collective-permute-start | bytes 1572872 | tf_op jit(solution)/shard_map/ppermute | solution.py:339
  12.5 3.5 %collective-permute-done.3.refs_0_ = bf16[64,4096]{1,0:T(8,128)(2,1)S(1)} collective-permute-done((bf16[64,4096]{1,0:T(8,128)(2,1)S(1)}, bf16[64,4096]{1,0:T(8,128)(2,1)S(1)}, u32[]{:S(2)}, u32[]{:S(2)}) %collective-permute-start.3) | collective-permute-done | bytes 524320 | tf_op jit(solution)/shard_map/ppermute | solution.py:339
  16.0 2.1 %collective-permute-start.7 = (bf16[64,4096]{1,0:T(8,128)(2,1)S(1)}, bf16[64,4096]{1,0:T(8,128)(2,1)S(1)}, u32[]{:S(2)}, u32[]{:S(2)}) collective-permute-start(bf16[64,4096]{1,0:T(8,128)(2,1)S(1)} %collective-permute-done.3.refs_0_), channel_id=1, source_target_pairs={{0,8},{8,16},{16,24},{24,28},{28,20},{20,12},{12,4},{4,0},{2,6},{1... | collective-permute-start | bytes 1572872 | tf_op jit(solution)/shard_map/ppermute | solution.py:339
  18.1 3.5 %collective-permute-done.5.refs_0_ = bf16[64,4096]{1,0:T(8,128)(2,1)S(1)} collective-permute-done((bf16[64,4096]{1,0:T(8,128)(2,1)S(1)}, bf16[64,4096]{1,0:T(8,128)(2,1)S(1)}, u32[]{:S(2)}, u32[]{:S(2)}) %collective-permute-start.5) | collective-permute-done | bytes 524320 | tf_op jit(solution)/shard_map/ppermute | solution.py:339
  21.6 2.1 %collective-permute-start.9 = (bf16[64,4096]{1,0:T(8,128)(2,1)S(1)}, bf16[64,4096]{1,0:T(8,128)(2,1)S(1)}, u32[]{:S(2)}, u32[]{:S(2)}) collective-permute-start(bf16[64,4096]{1,0:T(8,128)(2,1)S(1)} %collective-permute-done.5.refs_0_), channel_id=1, source_target_pairs={{0,8},{8,16},{16,24},{24,28},{28,20},{20,12},{12,4},{4,0},{2,6},{1... | collective-permute-start | bytes 1572872 | tf_op jit(solution)/shard_map/ppermute | solution.py:339
  23.7 0.0 collective-permute-start.2
  23.7 0.5 collective-permute-start.4
  24.2 3.0 %collective-permute-done.7.refs_2_ = bf16[64,4096]{1,0:T(8,128)(2,1)S(1)} collective-permute-done((bf16[64,4096]{1,0:T(8,128)(2,1)S(1)}, bf16[64,4096]{1,0:T(8,128)(2,1)S(1)}, u32[]{:S(2)}, u32[]{:S(2)}) %collective-permute-start.7) | collective-permute-done | bytes 524320 | tf_op jit(solution)/shard_map/ppermute | solution.py:339
  27.3 2.1 %collective-permute-start.11 = (bf16[64,4096]{1,0:T(8,128)(2,1)S(1)}, bf16[64,4096]{1,0:T(8,128)(2,1)S(1)}, u32[]{:S(2)}, u32[]{:S(2)}) collective-permute-start(bf16[64,4096]{1,0:T(8,128)(2,1)S(1)} %collective-permute-done.7.refs_2_), channel_id=1, source_target_pairs={{0,8},{8,16},{16,24},{24,28},{28,20},{20,12},{12,4},{4,0},{2,6},{1... | collective-permute-start | bytes 1572872 | tf_op jit(solution)/shard_map/ppermute | solution.py:339
  29.4 3.5 %collective-permute-done.9.refs_0_ = bf16[64,4096]{1,0:T(8,128)(2,1)S(1)} collective-permute-done((bf16[64,4096]{1,0:T(8,128)(2,1)S(1)}, bf16[64,4096]{1,0:T(8,128)(2,1)S(1)}, u32[]{:S(2)}, u32[]{:S(2)}) %collective-permute-start.9) | collective-permute-done | bytes 524320 | tf_op jit(solution)/shard_map/ppermute | solution.py:339
  32.9 2.1 %collective-permute-start.13 = (bf16[64,4096]{1,0:T(8,128)(2,1)S(1)}, bf16[64,4096]{1,0:T(8,128)(2,1)S(1)}, u32[]{:S(2)}, u32[]{:S(2)}) collective-permute-start(bf16[64,4096]{1,0:T(8,128)(2,1)S(1)} %collective-permute-done.9.refs_0_), channel_id=1, source_target_pairs={{0,8},{8,16},{16,24},{24,28},{28,20},{20,12},{12,4},{4,0},{2,6},{1... | collective-permute-start | bytes 1572872 | tf_op jit(solution)/shard_map/ppermute | solution.py:339
  35.0 0.0 collective-permute-start.6
  35.0 0.0 collective-permute-done.2.refs_3_
  35.0 0.5 collective-permute-start.8
  35.5 0.0 collective-permute-done.4.refs_1_
  35.5 0.1 collective-permute-start.10
  35.6 4.9 %shard_map.37 = (bf16[1024,4096]{1,0:T(8,128)(2,1)S(1)}, f32[8,128]{1,0:T(8,128)S(1)}) custom-call(bf16[1024,4096]{1,0:T(8,128)(2,1)} %grad_ref.1), custom_call_target="tpu_custom_call" | custom-call | flops 8388608 | bytes 8388608 | tf_op jit(solution)/shard_map/pallas_call | solution.py:200
  40.5 0.0 collective-permute-done.11.refs_0_
  40.5 0.5 collective-permute-start.12
  41.0 3.1 %collective-permute-done.13.refs_0_ = bf16[64,4096]{1,0:T(8,128)(2,1)S(1)} collective-permute-done((bf16[64,4096]{1,0:T(8,128)(2,1)S(1)}, bf16[64,4096]{1,0:T(8,128)(2,1)S(1)}, u32[]{:S(2)}, u32[]{:S(2)}) %collective-permute-start.13) | collective-permute-done | bytes 524320 | tf_op jit(solution)/shard_map/ppermute | solution.py:339
  44.1 0.0 collective-permute-start.14
  44.1 0.0 copy-done
  44.1 2.5 %shard_map.38 = (bf16[2,1024,128]{2,1,0:T(8,128)(2,1)S(1)}, bf16[1024,4096]{1,0:T(8,128)(2,1)S(1)}) custom-call(bf16[1024,4096]{1,0:T(8,128)(2,1)S(1)} %get-tuple-element.27.grad_ref, bf16[64,4096]{1,0:T(8,128)(2,1)S(1)} %copy-done, bf16[64,4096]{1,0:T(8,128)(2,1)S(1)} %collective-permute-done.refs_1_, ...), custom_call_target="tpu_custom_call", output_to_operand_aliasing={{1}: (0, {})} | custom-call | flops 2147483648 | bytes 8388608 | tf_op jit(solution)/shard_map/pallas_call | solution.py:153
  46.6 2.4 %shard_map.39 = (bf16[1,1024,128]{2,1,0:T(8,128)(2,1)S(1)}, bf16[1024,4096]{1,0:T(8,128)(2,1)S(1)}) custom-call(bf16[1024,4096]{1,0:T(8,128)(2,1)S(1)} %get-tuple-element.28.grad_ref, bf16[64,4096]{1,0:T(8,128)(2,1)S(1)} %collective-permute-done.3.refs_0_, bf16[64,4096]{1,0:T(8,128)(2,1)S(1)} %collective-permute-done.4.refs_1_), custom_call_target="tpu_custom_call", output_to_operand_aliasing={{1}: (0, {})} | custom-call | flops 1073741824 | bytes 8388608 | tf_op jit(solution)/shard_map/pallas_call | solution.py:153
  49.0 0.0 collective-permute-done.6.refs_1_
  49.0 0.0 collective-permute-done.8.refs_3_
  49.0 2.6 %shard_map.40 = (bf16[2,1024,128]{2,1,0:T(8,128)(2,1)S(1)}, bf16[1024,4096]{1,0:T(8,128)(2,1)S(1)}, bf16[1024,128]{1,0:T(8,128)(2,1)S(1)}) custom-call(bf16[1024,4096]{1,0:T(8,128)(2,1)S(1)} %get-tuple-element.29.grad_ref, bf16[64,4096]{1,0:T(8,128)(2,1)S(1)} %collective-permute-done.5.refs_0_, ...), custom_call_target="tpu_custom_call", output_to_operand_aliasing={{1}: (0, {})} | custom-call | flops 2147483648 | bytes 8388608 | tf_op jit(solution)/shard_map/pallas_call | solution.py:153
  51.6 0.0 collective-permute-done.10.refs_1_
  51.6 2.5 %shard_map.41 = (bf16[1,1024,128]{2,1,0:T(8,128)(2,1)S(1)}, bf16[1024,4096]{1,0:T(8,128)(2,1)S(1)}, bf16[1024,128]{1,0:T(8,128)(2,1)S(1)}) custom-call(bf16[1024,4096]{1,0:T(8,128)(2,1)S(1)} %get-tuple-element.32.grad_ref, bf16[64,4096]{1,0:T(8,128)(2,1)S(1)} %collective-permute-done.9.refs_0_, ...), custom_call_target="tpu_custom_call", output_to_operand_aliasing={{1}: (0, {})} | custom-call | flops 1073741824 | bytes 8388608 | tf_op jit(solution)/shard_map/pallas_call | solution.py:153
  54.1 2.1 %collective-permute-start.17 = (bf16[1024,128]{1,0:T(8,128)(2,1)S(1)}, bf16[1024,128]{1,0:T(8,128)(2,1)S(1)}, u32[]{:S(2)}, u32[]{:S(2)}) collective-permute-start(bf16[1024,128]{1,0:T(8,128)(2,1)S(1)} %get-tuple-element.40), channel_id=1, source_target_pairs={{0,1},{1,0},{2,3},{3,2},{4,5},{5,4},{6,7},{7,6},{8,9},{9,8},{10,11... | collective-permute-start | bytes 786440 | tf_op jit(solution)/shard_map/ppermute | solution.py:335
  56.2 0.1 collective-permute-start.16
  56.3 0.0 collective-permute-done.12.refs_1_
  56.3 2.7 %shard_map.42 = (bf16[1,1024,128]{2,1,0:T(8,128)(2,1)S(1)}, bf16[1024,4096]{1,0:T(8,128)(2,1)S(1)}, bf16[1024,128]{1,0:T(8,128)(2,1)S(1)}) custom-call(bf16[1024,4096]{1,0:T(8,128)(2,1)S(1)} %get-tuple-element.34.grad_ref, bf16[64,4096]{1,0:T(8,128)(2,1)S(1)} %collective-permute-done.11.refs_0_, ...), custom_call_target="tpu_custom_call", output_to_operand_aliasing={{1}: (0, {})} | custom-call | flops 1073741824 | bytes 8388608 | tf_op jit(solution)/shard_map/pallas_call | solution.py:153
  59.0 0.0 copy-start.1
  59.0 2.0 %collective-permute-start.18 = (bf16[1024,128]{1,0:T(8,128)(2,1)S(1)}, bf16[1024,128]{1,0:T(8,128)(2,1)S(1)}, u32[]{:S(2)}, u32[]{:S(2)}) collective-permute-start(bf16[1024,128]{1,0:T(8,128)(2,1)S(1)} %get-tuple-element.41), channel_id=1, source_target_pairs={{0,1},{1,0},{2,3},{3,2},{4,5},{5,4},{6,7},{7,6},{8,9},{9,8},{10,11... | collective-permute-start | bytes 786440 | tf_op jit(solution)/shard_map/ppermute | solution.py:335
  61.0 0.0 collective-permute-done.14.refs_1_
  61.0 2.5 %shard_map.43 = (bf16[1,1024,128]{2,1,0:T(8,128)(2,1)S(1)}, bf16[1024,4096]{1,0:T(8,128)(2,1)S(1)}, bf16[1024,128]{1,0:T(8,128)(2,1)S(1)}) custom-call(bf16[1024,4096]{1,0:T(8,128)(2,1)S(1)} %get-tuple-element.36.grad_ref, bf16[64,4096]{1,0:T(8,128)(2,1)S(1)} %collective-permute-done.13.refs_0_, ...), custom_call_target="tpu_custom_call", output_to_operand_aliasing={{1}: (0, {})} | custom-call | flops 1073741824 | bytes 8388608 | tf_op jit(solution)/shard_map/pallas_call | solution.py:153
  63.5 0.1 collective-permute-start.15
  63.7 1.9 %collective-permute-start.19 = (f32[8,128]{1,0:T(8,128)S(1)}, f32[8,128]{1,0:T(8,128)S(1)}, u32[]{:S(2)}, u32[]{:S(2)}) collective-permute-start(f32[8,128]{1,0:T(8,128)S(1)} %get-tuple-element.42.refs_3_), channel_id=1, source_target_pairs={{0,1},{1,0},{2,3},{3,2},{4,5},{5,4},{6,7},{7,6},{8,9},{9,8},{10,11... | collective-permute-start | bytes 12296 | tf_op jit(solution)/shard_map/ppermute | solution.py:335
  65.6 14.5 %collective-permute-done.19.refs_4_ = f32[8,128]{1,0:T(8,128)S(1)} collective-permute-done((f32[8,128]{1,0:T(8,128)S(1)}, f32[8,128]{1,0:T(8,128)S(1)}, u32[]{:S(2)}, u32[]{:S(2)}) %collective-permute-start.19) | collective-permute-done | bytes 4128 | tf_op jit(solution)/shard_map/ppermute | solution.py:335
  80.1 0.0 collective-permute-done.17.refs_1_
  80.1 0.0 collective-permute-done.16.refs_0_
  80.1 0.0 collective-permute-done.18.refs_2_
  80.1 0.0 copy-done.1
  80.1 1.5 %shard_map.44 = (f32[3,1024,128]{2,1,0:T(8,128)S(1)}, f32[3,2,128]{2,1,0:T(2,128)S(1)}, f32[1024,1]{1,0:T(8,128)S(1)}) custom-call(bf16[1024,128]{1,0:T(8,128)(2,1)S(1)} %collective-permute-done.16.refs_0_, bf16[1024,128]{1,0:T(8,128)(2,1)S(1)} %collective-permute-done.17.refs_1_, bf16[1024,128]{1,0:T(8,128)(2,1)S(1)} %collective-permute-done.18.refs_2_, ...), custom_call_target="tpu_custom_call" | custom-call | flops 3145728 | bytes 4718592 | tf_op jit(solution)/shard_map/pallas_call | solution.py:267
  81.6 0.0 collective-permute-done.15.refs_0_
  81.6 0.5 shard_map.45
  82.1 1.8 %collective-permute-start.20 = (f32[2,512]{1,0:T(2,128)S(1)}, f32[2,512]{1,0:T(2,128)S(1)}, u32[]{:S(2)}, u32[]{:S(2)}) collective-permute-start(f32[2,512]{1,0:T(2,128)S(1)} %get-tuple-element.46), channel_id=1, source_target_pairs={{0,2},{4,6},{8,10},{12,14},{16,18},{20,22},{24,26},{28,30},{1,3},{... | collective-permute-start | bytes 12296 | tf_op jit(solution)/shard_map/ppermute | solution.py:370
  83.9 0.8 collective-permute-done.20
  84.7 0.7 collective-permute-start.21
  85.4 0.0 collective-permute-done.21
  85.4 0.7 collective-permute-start.22
  86.1 0.0 collective-permute-done.22
  86.2 0.7 collective-permute-start.23
  86.8 0.0 collective-permute-done.23
  86.9 1.3 %collective-permute-start.24 = (f32[2,512]{1,0:T(2,128)S(1)}, f32[2,512]{1,0:T(2,128)S(1)}, u32[]{:S(2)}, u32[]{:S(2)}) collective-permute-start(f32[2,512]{1,0:T(2,128)S(1)} %pad_maximum_fusion.3.own_ref), channel_id=1, source_target_pairs={{2,0},{6,4},{10,8},{14,12},{18,16},{22,20},{26,24},{30,28},{3,1},{... | collective-permute-start | bytes 12296 | tf_op jit(solution)/shard_map/ppermute | solution.py:376
  88.2 12.9 %collective-permute-done.24.back_ref = f32[2,512]{1,0:T(2,128)S(1)} collective-permute-done((f32[2,512]{1,0:T(2,128)S(1)}, f32[2,512]{1,0:T(2,128)S(1)}, u32[]{:S(2)}, u32[]{:S(2)}) %collective-permute-start.24) | collective-permute-done | bytes 4128 | tf_op jit(solution)/shard_map/ppermute | solution.py:376
  101.1 1.5 %shard_map.46 = bf16[1024,512]{1,0:T(8,128)(2,1)} custom-call(f32[2,512]{1,0:T(2,128)S(1)} %pad_maximum_fusion.3.own_ref, f32[2,512]{1,0:T(2,128)S(1)} %collective-permute-done.24.back_ref, f32[3,1024,128]{2,1,0:T(8,128)S(1)} %get-tuple-element.47.early_ref, f32[1,1024,128]{2,1,0:T(8,128)S(1)} %get-tuple-element.48.late_ref), custom_call_target="tpu_custom_call" | custom-call | flops 1048576 | bytes 3145728 | tf_op jit(solution)/shard_map/pallas_call | solution.py:298
  (8 shorter events, 0.1 us)
Async XLA Ops:
  0.0 44.1 %copy-start = (bf16[64,4096]{1,0:T(8,128)(2,1)S(1)}, bf16[64,4096]{1,0:T(8,128)(2,1)}, u32[]{:S(2)}) copy-start(bf16[64,4096]{1,0:T(8,128)(2,1)} %refs_0_.1) | copy-start | bytes 1572868
  0.0 3.1 %collective-permute-start = (bf16[64,4096]{1,0:T(8,128)(2,1)}, bf16[64,4096]{1,0:T(8,128)(2,1)S(1)}, u32[]{:S(2)}, u32[]{:S(2)}) collective-permute-start(bf16[64,4096]{1,0:T(8,128)(2,1)} %refs_0_.1), channel_id=1, source_target_pairs={{0,2},{2,0},{4,6},{6,4},{8,10},{10,8},{12,14},{14,12},{16,18},{18,... | collective-permute-start | bytes 1572872 | tf_op jit(solution)/shard_map/ppermute | solution.py:337
  0.5 9.9 %collective-permute-start.1 = (bf16[64,4096]{1,0:T(8,128)(2,1)}, bf16[64,4096]{1,0:T(8,128)(2,1)S(1)}, u32[]{:S(2)}, u32[]{:S(2)}) collective-permute-start(bf16[64,4096]{1,0:T(8,128)(2,1)} %refs_0_.1), channel_id=1, source_target_pairs={{0,8},{8,16},{16,24},{24,28},{28,20},{20,12},{12,4},{4,0},{2,6},{1... | collective-permute-start | bytes 1572872 | tf_op jit(solution)/shard_map/ppermute | solution.py:339
  3.1 12.9 %collective-permute-start.3 = (bf16[64,4096]{1,0:T(8,128)(2,1)S(1)}, bf16[64,4096]{1,0:T(8,128)(2,1)S(1)}, u32[]{:S(2)}, u32[]{:S(2)}) collective-permute-start(bf16[64,4096]{1,0:T(8,128)(2,1)S(1)} %collective-permute-done.refs_1_), channel_id=1, source_target_pairs={{0,8},{8,16},{16,24},{24,28},{28,20},{20,12},{12,4},{4,0},{2,6},{1... | collective-permute-start | bytes 1572872 | tf_op jit(solution)/shard_map/ppermute | solution.py:339
  10.4 11.2 %collective-permute-start.5 = (bf16[64,4096]{1,0:T(8,128)(2,1)S(1)}, bf16[64,4096]{1,0:T(8,128)(2,1)S(1)}, u32[]{:S(2)}, u32[]{:S(2)}) collective-permute-start(bf16[64,4096]{1,0:T(8,128)(2,1)S(1)} %collective-permute-done.1.refs_2_), channel_id=1, source_target_pairs={{0,8},{8,16},{16,24},{24,28},{28,20},{20,12},{12,4},{4,0},{2,6},{1... | collective-permute-start | bytes 1572872 | tf_op jit(solution)/shard_map/ppermute | solution.py:339
  16.0 11.2 %collective-permute-start.7 = (bf16[64,4096]{1,0:T(8,128)(2,1)S(1)}, bf16[64,4096]{1,0:T(8,128)(2,1)S(1)}, u32[]{:S(2)}, u32[]{:S(2)}) collective-permute-start(bf16[64,4096]{1,0:T(8,128)(2,1)S(1)} %collective-permute-done.3.refs_0_), channel_id=1, source_target_pairs={{0,8},{8,16},{16,24},{24,28},{28,20},{20,12},{12,4},{4,0},{2,6},{1... | collective-permute-start | bytes 1572872 | tf_op jit(solution)/shard_map/ppermute | solution.py:339
  21.6 11.2 %collective-permute-start.9 = (bf16[64,4096]{1,0:T(8,128)(2,1)S(1)}, bf16[64,4096]{1,0:T(8,128)(2,1)S(1)}, u32[]{:S(2)}, u32[]{:S(2)}) collective-permute-start(bf16[64,4096]{1,0:T(8,128)(2,1)S(1)} %collective-permute-done.5.refs_0_), channel_id=1, source_target_pairs={{0,8},{8,16},{16,24},{24,28},{28,20},{20,12},{12,4},{4,0},{2,6},{1... | collective-permute-start | bytes 1572872 | tf_op jit(solution)/shard_map/ppermute | solution.py:339
  23.7 11.2 %collective-permute-start.2 = (bf16[64,4096]{1,0:T(8,128)(2,1)S(1)}, bf16[64,4096]{1,0:T(8,128)(2,1)S(1)}, u32[]{:S(2)}, u32[]{:S(2)}) collective-permute-start(bf16[64,4096]{1,0:T(8,128)(2,1)S(1)} %collective-permute-done.1.refs_2_), channel_id=1, source_target_pairs={{0,2},{2,0},{4,6},{6,4},{8,10},{10,8},{12,14},{14,12},{16,18},{18,... | collective-permute-start | bytes 1572872 | tf_op jit(solution)/shard_map/ppermute | solution.py:342
  23.7 11.8 %collective-permute-start.4 = (bf16[64,4096]{1,0:T(8,128)(2,1)S(1)}, bf16[64,4096]{1,0:T(8,128)(2,1)S(1)}, u32[]{:S(2)}, u32[]{:S(2)}) collective-permute-start(bf16[64,4096]{1,0:T(8,128)(2,1)S(1)} %collective-permute-done.3.refs_0_), channel_id=1, source_target_pairs={{0,2},{2,0},{4,6},{6,4},{8,10},{10,8},{12,14},{14,12},{16,18},{18,... | collective-permute-start | bytes 1572872 | tf_op jit(solution)/shard_map/ppermute | solution.py:342
  27.3 13.2 %collective-permute-start.11 = (bf16[64,4096]{1,0:T(8,128)(2,1)S(1)}, bf16[64,4096]{1,0:T(8,128)(2,1)S(1)}, u32[]{:S(2)}, u32[]{:S(2)}) collective-permute-start(bf16[64,4096]{1,0:T(8,128)(2,1)S(1)} %collective-permute-done.7.refs_2_), channel_id=1, source_target_pairs={{0,8},{8,16},{16,24},{24,28},{28,20},{20,12},{12,4},{4,0},{2,6},{1... | collective-permute-start | bytes 1572872 | tf_op jit(solution)/shard_map/ppermute | solution.py:339
  32.9 11.2 %collective-permute-start.13 = (bf16[64,4096]{1,0:T(8,128)(2,1)S(1)}, bf16[64,4096]{1,0:T(8,128)(2,1)S(1)}, u32[]{:S(2)}, u32[]{:S(2)}) collective-permute-start(bf16[64,4096]{1,0:T(8,128)(2,1)S(1)} %collective-permute-done.9.refs_0_), channel_id=1, source_target_pairs={{0,8},{8,16},{16,24},{24,28},{28,20},{20,12},{12,4},{4,0},{2,6},{1... | collective-permute-start | bytes 1572872 | tf_op jit(solution)/shard_map/ppermute | solution.py:339
  35.0 14.0 %collective-permute-start.6 = (bf16[64,4096]{1,0:T(8,128)(2,1)S(1)}, bf16[64,4096]{1,0:T(8,128)(2,1)S(1)}, u32[]{:S(2)}, u32[]{:S(2)}) collective-permute-start(bf16[64,4096]{1,0:T(8,128)(2,1)S(1)} %collective-permute-done.5.refs_0_), channel_id=1, source_target_pairs={{0,2},{2,0},{4,6},{6,4},{8,10},{10,8},{12,14},{14,12},{16,18},{18,... | collective-permute-start | bytes 1572872 | tf_op jit(solution)/shard_map/ppermute | solution.py:342
  35.0 14.0 %collective-permute-start.8 = (bf16[64,4096]{1,0:T(8,128)(2,1)S(1)}, bf16[64,4096]{1,0:T(8,128)(2,1)S(1)}, u32[]{:S(2)}, u32[]{:S(2)}) collective-permute-start(bf16[64,4096]{1,0:T(8,128)(2,1)S(1)} %collective-permute-done.7.refs_2_), channel_id=1, source_target_pairs={{0,2},{2,0},{4,6},{6,4},{8,10},{10,8},{12,14},{14,12},{16,18},{18,... | collective-permute-start | bytes 1572872 | tf_op jit(solution)/shard_map/ppermute | solution.py:342
  35.5 16.1 %collective-permute-start.10 = (bf16[64,4096]{1,0:T(8,128)(2,1)S(1)}, bf16[64,4096]{1,0:T(8,128)(2,1)S(1)}, u32[]{:S(2)}, u32[]{:S(2)}) collective-permute-start(bf16[64,4096]{1,0:T(8,128)(2,1)S(1)} %collective-permute-done.9.refs_0_), channel_id=1, source_target_pairs={{0,2},{2,0},{4,6},{6,4},{8,10},{10,8},{12,14},{14,12},{16,18},{18,... | collective-permute-start | bytes 1572872 | tf_op jit(solution)/shard_map/ppermute | solution.py:342
  40.5 15.8 %collective-permute-start.12 = (bf16[64,4096]{1,0:T(8,128)(2,1)S(1)}, bf16[64,4096]{1,0:T(8,128)(2,1)S(1)}, u32[]{:S(2)}, u32[]{:S(2)}) collective-permute-start(bf16[64,4096]{1,0:T(8,128)(2,1)S(1)} %collective-permute-done.11.refs_0_), channel_id=1, source_target_pairs={{0,2},{2,0},{4,6},{6,4},{8,10},{10,8},{12,14},{14,12},{16,18},{18,... | collective-permute-start | bytes 1572872 | tf_op jit(solution)/shard_map/ppermute | solution.py:342
  44.1 16.9 %collective-permute-start.14 = (bf16[64,4096]{1,0:T(8,128)(2,1)S(1)}, bf16[64,4096]{1,0:T(8,128)(2,1)S(1)}, u32[]{:S(2)}, u32[]{:S(2)}) collective-permute-start(bf16[64,4096]{1,0:T(8,128)(2,1)S(1)} %collective-permute-done.13.refs_0_), channel_id=1, source_target_pairs={{0,2},{2,0},{4,6},{6,4},{8,10},{10,8},{12,14},{14,12},{16,18},{18,... | collective-permute-start | bytes 1572872 | tf_op jit(solution)/shard_map/ppermute | solution.py:342
  54.1 26.0 %collective-permute-start.17 = (bf16[1024,128]{1,0:T(8,128)(2,1)S(1)}, bf16[1024,128]{1,0:T(8,128)(2,1)S(1)}, u32[]{:S(2)}, u32[]{:S(2)}) collective-permute-start(bf16[1024,128]{1,0:T(8,128)(2,1)S(1)} %get-tuple-element.40), channel_id=1, source_target_pairs={{0,1},{1,0},{2,3},{3,2},{4,5},{5,4},{6,7},{7,6},{8,9},{9,8},{10,11... | collective-permute-start | bytes 786440 | tf_op jit(solution)/shard_map/ppermute | solution.py:335
  56.2 23.9 %collective-permute-start.16 = (bf16[1024,128]{1,0:T(8,128)(2,1)S(1)}, bf16[1024,128]{1,0:T(8,128)(2,1)S(1)}, u32[]{:S(2)}, u32[]{:S(2)}) collective-permute-start(bf16[1024,128]{1,0:T(8,128)(2,1)S(1)} %get-tuple-element.39), channel_id=1, source_target_pairs={{0,1},{1,0},{2,3},{3,2},{4,5},{5,4},{6,7},{7,6},{8,9},{9,8},{10,11... | collective-permute-start | bytes 786440 | tf_op jit(solution)/shard_map/ppermute | solution.py:335
  59.0 21.1 %copy-start.1 = (f32[1024]{0:T(1024)S(1)}, f32[1024]{0:T(1024)}, u32[]{:S(2)}) copy-start(f32[1024]{0:T(1024)} %param.5) | copy-start | bytes 12292
  59.0 21.1 %collective-permute-start.18 = (bf16[1024,128]{1,0:T(8,128)(2,1)S(1)}, bf16[1024,128]{1,0:T(8,128)(2,1)S(1)}, u32[]{:S(2)}, u32[]{:S(2)}) collective-permute-start(bf16[1024,128]{1,0:T(8,128)(2,1)S(1)} %get-tuple-element.41), channel_id=1, source_target_pairs={{0,1},{1,0},{2,3},{3,2},{4,5},{5,4},{6,7},{7,6},{8,9},{9,8},{10,11... | collective-permute-start | bytes 786440 | tf_op jit(solution)/shard_map/ppermute | solution.py:335
  63.5 18.1 %collective-permute-start.15 = (bf16[1024,128]{1,0:T(8,128)(2,1)S(1)}, bf16[1024,128]{1,0:T(8,128)(2,1)S(1)}, u32[]{:S(2)}, u32[]{:S(2)}) collective-permute-start(bf16[1024,128]{1,0:T(8,128)(2,1)S(1)} %get-tuple-element.38), channel_id=1, source_target_pairs={{0,1},{1,0},{2,3},{3,2},{4,5},{5,4},{6,7},{7,6},{8,9},{9,8},{10,11... | collective-permute-start | bytes 786440 | tf_op jit(solution)/shard_map/ppermute | solution.py:335
  63.7 16.4 %collective-permute-start.19 = (f32[8,128]{1,0:T(8,128)S(1)}, f32[8,128]{1,0:T(8,128)S(1)}, u32[]{:S(2)}, u32[]{:S(2)}) collective-permute-start(f32[8,128]{1,0:T(8,128)S(1)} %get-tuple-element.42.refs_3_), channel_id=1, source_target_pairs={{0,1},{1,0},{2,3},{3,2},{4,5},{5,4},{6,7},{7,6},{8,9},{9,8},{10,11... | collective-permute-start | bytes 12296 | tf_op jit(solution)/shard_map/ppermute | solution.py:335
  82.1 2.6 %collective-permute-start.20 = (f32[2,512]{1,0:T(2,128)S(1)}, f32[2,512]{1,0:T(2,128)S(1)}, u32[]{:S(2)}, u32[]{:S(2)}) collective-permute-start(f32[2,512]{1,0:T(2,128)S(1)} %get-tuple-element.46), channel_id=1, source_target_pairs={{0,2},{4,6},{8,10},{12,14},{16,18},{20,22},{24,26},{28,30},{1,3},{... | collective-permute-start | bytes 12296 | tf_op jit(solution)/shard_map/ppermute | solution.py:370
  84.7 0.7 collective-permute-start.21
  85.4 0.7 collective-permute-start.22
  86.2 0.7 collective-permute-start.23
  86.9 14.2 %collective-permute-start.24 = (f32[2,512]{1,0:T(2,128)S(1)}, f32[2,512]{1,0:T(2,128)S(1)}, u32[]{:S(2)}, u32[]{:S(2)}) collective-permute-start(f32[2,512]{1,0:T(2,128)S(1)} %pad_maximum_fusion.3.own_ref), channel_id=1, source_target_pairs={{2,0},{6,4},{10,8},{14,12},{18,16},{22,20},{26,24},{30,28},{3,1},{... | collective-permute-start | bytes 12296 | tf_op jit(solution)/shard_map/ppermute | solution.py:376

commit v2 on v1

--- a/solution.py
+++ b/solution.py
@@ -47,12 +47,7 @@
         self.order = ring_order(planes)
         self.nodes = len(self.order)
         self.far = self.nodes // 2
-        low, high = [0], [0]
-        for s in range(1, self.far):
-            low += [-s, s]
-            high += [s, -s]
-        self.offsets = (low + [self.far], high + [self.far])
-        self.pairs = len(self.offsets[0])
+        self.pairs = 2 * self.far
         self.turns = self.pairs // 2
         self.give, self.take, self.place = {}, {}, {}
         for n, (z, x) in enumerate(self.order):
@@ -61,7 +56,7 @@
                 for half in range(2):
                     mine, other = [], []
                     spot = [0] * self.turns
-                    for p, o in enumerate(self.offsets[half]):
+                    for p, o in enumerate(self.offsets(n, half)):
                         oz, ox = self.order[(n + o) % self.nodes]
                         chip = oz * 2 + ox
                         if chip // self.turns == f:
@@ -72,6 +67,13 @@
                     self.give[key, half] = other
                     self.take[key, half] = mine
                     self.place[key, half] = spot
+
+    def offsets(self, n, half):
+        out = [0]
+        for s in range(1, self.far):
+            first = -s if (n + s + half) % 2 == 0 else s
+            out += [first, -first]
+        return out + [self.far]
 
     def packed(self, table, half):
         key = (lax.axis_index("rows") // 2) * 2 + lax.axis_index("feat")
@@ -275,34 +277,49 @@
     )(*args)
 
 
-def finish_kernel(plan, count, own_ref, back_ref, early_ref, late_ref, out_ref):
+def arrange_kernel(plan, early_ref, late_ref, out_ref):
     lane = lax.broadcasted_iota(jnp.int32, late_ref.shape[1:], 1)
     codes = [plan.packed(plan.place, half) for half in range(2)]
     early = early_ref.shape[0]
-    stat = jnp.where(lax.axis_index("rows") % 2 == 1, own_ref[...], back_ref[...])
-    mean, scale = stat[0:1, :], lax.rsqrt(stat[1:2, :] / count + VAR_EPS)
     for j in range(plan.turns):
         halves = []
         for half in range(2):
             index = entry(codes[half], j)
             value = early_ref[jnp.minimum(index, early - 1)]
             halves.append(jnp.where(index < early, value, late_ref[0]))
-        value = jnp.where(lane < 64, halves[0], halves[1])
-        columns = slice(j * 128, (j + 1) * 128)
-        out_ref[:, columns] = ((value - mean[:, columns]) * scale[:, columns]).astype(jnp.bfloat16)
-
-
-def finish_call(plan, count, own, back, early, late):
-    rows = late.shape[1]
-    width = plan.turns * 128
+        out_ref[:, j * 128:(j + 1) * 128] = jnp.where(lane < 64, halves[0], halves[1])
+
+
+def arrange_call(plan, early, late):
+    rows, width = late.shape[1], plan.turns * 128
     return pl.pallas_call(
-        functools.partial(finish_kernel, plan, count),
-        out_shape=jax.ShapeDtypeStruct((rows, width), jnp.bfloat16),
-        in_specs=[VMEM] * 4,
+        functools.partial(arrange_kernel, plan),
+        out_shape=jax.ShapeDtypeStruct((rows, width), jnp.float32),
+        in_specs=[VMEM] * 2,
         out_specs=VMEM,
         compiler_params=pltpu.CompilerParams(vmem_limit_bytes=8 * 1024 * 1024),
+        cost_estimate=pl.CostEstimate(flops=rows * width, bytes_accessed=8 * rows * width, transcendentals=0),
+    )(early, late)
+
+
+def finish_kernel(count, stat_ref, scored_ref, out_ref):
+    rows = out_ref.shape[0]
+    here = pl.ds(pl.multiple_of(pl.program_id(0) * rows, rows), rows)
+    scale = lax.rsqrt(stat_ref[1:2, :] / count + VAR_EPS)
+    out_ref[...] = ((scored_ref[here, :] - stat_ref[0:1, :]) * scale).astype(jnp.bfloat16)
+
+
+def finish_call(count, stat, scored, steps=4):
+    rows, width = scored.shape
+    return pl.pallas_call(
+        functools.partial(finish_kernel, count),
+        grid=(steps,),
+        out_shape=jax.ShapeDtypeStruct((rows, width), jnp.bfloat16),
+        in_specs=[VMEM] * 2,
+        out_specs=pl.BlockSpec((rows // steps, width), lambda i: (i, 0)),
+        compiler_params=pltpu.CompilerParams(vmem_limit_bytes=8 * 1024 * 1024),
         cost_estimate=pl.CostEstimate(flops=2 * rows * width, bytes_accessed=6 * rows * width, transcendentals=0),
-    )(own, back, early, late)
+    )(stat, scored)
 
 
 def product_groups(plan):
@@ -328,8 +345,8 @@
         return (z * 2 + x) * 2 + c
 
     swap = [(r, r ^ 1) for r in range(2 * nodes)]
-    turn = [(device(n, 0), device(n + 1, 0)) for n in range(nodes)]
-    turn += [(device(n, 1), device(n - 1, 1)) for n in range(nodes)]
+    turn = [(device(n, n % 2), device(n + 1, (n + 1) % 2)) for n in range(nodes)]
+    turn += [(device(n, 1 - n % 2), device(n - 1, n % 2)) for n in range(nodes)]
 
     def cross(value):
         return lax.ppermute(value, "feat", [(0, 1), (1, 0)])
@@ -339,7 +356,8 @@
         ring.append(lax.ppermute(ring[-2], "rows", turn))
     arrived = [([queries, ring[1]], [True, False])]
     for k in range(1, 2 * far):
-        arrived.append(([ring[k + 1], lax.ppermute(ring[k + 1], "rows", swap)], [k % 2 == 1, k % 2 == 0]))
+        same = [(k + 1) // 2 % 2 == 0, (k + 1) // 2 % 2 == 1]
+        arrived.append(([ring[k + 1], lax.ppermute(ring[k + 1], "rows", swap)], same if k % 2 else same[::-1]))
 
     gradients, squares = load_call(gradients)
     squares = (squares, cross(squares), loss_weight.reshape(rows_here // 128, 128))
@@ -358,23 +376,18 @@
     early, stat, factor = score_call(plan, list(range(last)), comes[:last], known, feature_count, squares)
     late, stat = score_call(plan, [last], comes[last:], known, feature_count, None, factor, stat)
 
-    chips = [r for r in range(2 * nodes) if r % 2 == 1]
-    ways = [[(r - 1, r) for r in chips]]
-    step = 2
+    scored = arrange_call(plan, early, late)
+    mean, spread = stat[0:1], stat[1:2]
+    count, step = rows_here, 1
     while step < 2 * nodes:
-        ways.append([(r, r ^ step) for r in chips])
-        step *= 2
-    mean, spread = stat[0:1], stat[1:2]
-    count = rows_here
-    for pairs in ways:
+        pairs = [(r, r ^ (step | 1)) for r in range(2 * nodes)]
         come = lax.ppermute(jnp.concatenate([mean, spread], axis=0), "rows", pairs)
         gap = come[0:1] - mean
         mean = 0.5 * (mean + come[0:1])
         spread = spread + come[1:2] + (0.5 * count) * (gap * gap)
         count *= 2
-    stat = jnp.concatenate([mean, spread], axis=0)
-    back = lax.ppermute(stat, "rows", [(r, r - 1) for r in chips])
-    return finish_call(plan, count, stat, back, early, late)
+        step *= 2
+    return finish_call(count, jnp.concatenate([mean, spread], axis=0), scored)
 
 
 def solution(mesh):

time: 103 us -> 94.7 us (0.919)
  waiting for transfers between devices: 50.2 us -> 41.2 us
    ppermute x1 -> x0, waiting for transfers between devices: 12.9 us -> none  [ring_body(): back = lax.ppermute(stat, 'rows', [(r, r - 1) for r in chips])]
    ppermute x4, waiting for transfers between devices: 0.81 us -> 5.19 us  [ring_body(): come = lax.ppermute(jnp.concatenate([mean, spread], axis=0), 'rows', pairs)]
    ppermute x4, starting transfers between devices: 3.8 us -> 5.85 us  [ring_body(): come = lax.ppermute(jnp.concatenate([mean, spread], axis=0), 'rows', pairs)]
    ppermute x1 -> x0, starting transfers between devices: 1.29 us -> none  [ring_body(): back = lax.ppermute(stat, 'rows', [(r, r - 1) for r in chips])]
  transfers between devices with their start and end apart: 25 -> 24, of which waited for: 9 -> 11; matrix products, arithmetic and copies ran while one was open for 0% -> 0% of each run, Pallas kernels for 21% -> 23%
where the time goes in v2:
time: 94.7 us; the launch traced here: 94.6 us
  waiting for transfers between devices  41.2 us (44%)
  starting transfers between devices  29.3 us (31%)
  Pallas kernels  23.8 us (25%)
    ppermute x7, waiting for transfers between devices, ring_body(): ring.append(lax.ppermute(ring[-2], 'rows', turn))  21.8 us
    pallas_call x6, Pallas kernels, product_call(): pl.pallas_call(functools.partial(product_kernel, plan, sources, count, tu...  15 us
    ppermute x7, starting transfers between devices, ring_body(): ring.append(lax.ppermute(ring[-2], 'rows', turn))  15 us
    ppermute x5, waiting for transfers between devices, cross(): return lax.ppermute(value, 'feat', [(0, 1), (1, 0)])  14.2 us
    ppermute x5, starting transfers between devices, cross(): return lax.ppermute(value, 'feat', [(0, 1), (1, 0)])  6.21 us
    ppermute x4, starting transfers between devices, ring_body(): come = lax.ppermute(jnp.concatenate([mean, spread], axis=0), 'rows', pairs)  5.85 us
    ppermute x4, waiting for transfers between devices, ring_body(): come = lax.ppermute(jnp.concatenate([mean, spread], axis=0), 'rows', pairs)  5.19 us
    pallas_call x1, Pallas kernels, load_call(): pl.pallas_call(functools.partial(load_kernel, parts), out_shape=[jax.Shap...  4.9 us
  transfers between devices with their start and end apart: 24, of which 11 were waited for; matrix products, arithmetic and copies ran while one was open for 0% of the time, Pallas kernels for 23%

profile of v2, /device:TPU:0, one launch (start us, length us, event | category | flops | bytes accessed | tf_op | source)
XLA Modules:
  0.0 94.6 jit_solution(10496345539625100597)
XLA Ops:
  0.0 0.0 copy-start
  0.0 0.5 collective-permute-start
  0.5 2.7 %collective-permute-start.1 = (bf16[64,4096]{1,0:T(8,128)(2,1)}, bf16[64,4096]{1,0:T(8,128)(2,1)S(1)}, u32[]{:S(2)}, u32[]{:S(2)}) collective-permute-start(bf16[64,4096]{1,0:T(8,128)(2,1)} %refs_0_.1), channel_id=1, source_target_pairs={{0,10},{10,16},{16,26},{26,28},{28,22},{22,12},{12,6},{6,0},{2,4},... | collective-permute-start | bytes 1572872 | tf_op jit(solution)/shard_map/ppermute | solution.py:356
  3.2 0.0 collective-permute-done.refs_1_
  3.2 1.7 %collective-permute-start.3 = (bf16[64,4096]{1,0:T(8,128)(2,1)S(1)}, bf16[64,4096]{1,0:T(8,128)(2,1)S(1)}, u32[]{:S(2)}, u32[]{:S(2)}) collective-permute-start(bf16[64,4096]{1,0:T(8,128)(2,1)S(1)} %collective-permute-done.refs_1_), channel_id=1, source_target_pairs={{0,10},{10,16},{16,26},{26,28},{28,22},{22,12},{12,6},{6,0},{2,4},... | collective-permute-start | bytes 1572872 | tf_op jit(solution)/shard_map/ppermute | solution.py:356
  4.9 5.3 %collective-permute-done.1.refs_2_ = bf16[64,4096]{1,0:T(8,128)(2,1)S(1)} collective-permute-done((bf16[64,4096]{1,0:T(8,128)(2,1)}, bf16[64,4096]{1,0:T(8,128)(2,1)S(1)}, u32[]{:S(2)}, u32[]{:S(2)}) %collective-permute-start.1) | collective-permute-done | bytes 524320 | tf_op jit(solution)/shard_map/ppermute | solution.py:356
  10.2 2.1 %collective-permute-start.5 = (bf16[64,4096]{1,0:T(8,128)(2,1)S(1)}, bf16[64,4096]{1,0:T(8,128)(2,1)S(1)}, u32[]{:S(2)}, u32[]{:S(2)}) collective-permute-start(bf16[64,4096]{1,0:T(8,128)(2,1)S(1)} %collective-permute-done.1.refs_2_), channel_id=1, source_target_pairs={{0,10},{10,16},{16,26},{26,28},{28,22},{22,12},{12,6},{6,0},{2,4},... | collective-permute-start | bytes 1572872 | tf_op jit(solution)/shard_map/ppermute | solution.py:356
  12.3 3.5 %collective-permute-done.3.refs_0_ = bf16[64,4096]{1,0:T(8,128)(2,1)S(1)} collective-permute-done((bf16[64,4096]{1,0:T(8,128)(2,1)S(1)}, bf16[64,4096]{1,0:T(8,128)(2,1)S(1)}, u32[]{:S(2)}, u32[]{:S(2)}) %collective-permute-start.3) | collective-permute-done | bytes 524320 | tf_op jit(solution)/shard_map/ppermute | solution.py:356
  15.8 2.1 %collective-permute-start.7 = (bf16[64,4096]{1,0:T(8,128)(2,1)S(1)}, bf16[64,4096]{1,0:T(8,128)(2,1)S(1)}, u32[]{:S(2)}, u32[]{:S(2)}) collective-permute-start(bf16[64,4096]{1,0:T(8,128)(2,1)S(1)} %collective-permute-done.3.refs_0_), channel_id=1, source_target_pairs={{0,10},{10,16},{16,26},{26,28},{28,22},{22,12},{12,6},{6,0},{2,4},... | collective-permute-start | bytes 1572872 | tf_op jit(solution)/shard_map/ppermute | solution.py:356
  17.9 3.5 %collective-permute-done.5.refs_0_ = bf16[64,4096]{1,0:T(8,128)(2,1)S(1)} collective-permute-done((bf16[64,4096]{1,0:T(8,128)(2,1)S(1)}, bf16[64,4096]{1,0:T(8,128)(2,1)S(1)}, u32[]{:S(2)}, u32[]{:S(2)}) %collective-permute-start.5) | collective-permute-done | bytes 524320 | tf_op jit(solution)/shard_map/ppermute | solution.py:356
  21.4 2.1 %collective-permute-start.9 = (bf16[64,4096]{1,0:T(8,128)(2,1)S(1)}, bf16[64,4096]{1,0:T(8,128)(2,1)S(1)}, u32[]{:S(2)}, u32[]{:S(2)}) collective-permute-start(bf16[64,4096]{1,0:T(8,128)(2,1)S(1)} %collective-permute-done.5.refs_0_), channel_id=1, source_target_pairs={{0,10},{10,16},{16,26},{26,28},{28,22},{22,12},{12,6},{6,0},{2,4},... | collective-permute-start | bytes 1572872 | tf_op jit(solution)/shard_map/ppermute | solution.py:356
  23.5 0.0 collective-permute-start.2
  23.5 0.5 collective-permute-start.4
  24.0 3.0 %collective-permute-done.7.refs_2_ = bf16[64,4096]{1,0:T(8,128)(2,1)S(1)} collective-permute-done((bf16[64,4096]{1,0:T(8,128)(2,1)S(1)}, bf16[64,4096]{1,0:T(8,128)(2,1)S(1)}, u32[]{:S(2)}, u32[]{:S(2)}) %collective-permute-start.7) | collective-permute-done | bytes 524320 | tf_op jit(solution)/shard_map/ppermute | solution.py:356
  27.0 2.1 %collective-permute-start.11 = (bf16[64,4096]{1,0:T(8,128)(2,1)S(1)}, bf16[64,4096]{1,0:T(8,128)(2,1)S(1)}, u32[]{:S(2)}, u32[]{:S(2)}) collective-permute-start(bf16[64,4096]{1,0:T(8,128)(2,1)S(1)} %collective-permute-done.7.refs_2_), channel_id=1, source_target_pairs={{0,10},{10,16},{16,26},{26,28},{28,22},{22,12},{12,6},{6,0},{2,4},... | collective-permute-start | bytes 1572872 | tf_op jit(solution)/shard_map/ppermute | solution.py:356
  29.1 3.5 %collective-permute-done.9.refs_0_ = bf16[64,4096]{1,0:T(8,128)(2,1)S(1)} collective-permute-done((bf16[64,4096]{1,0:T(8,128)(2,1)S(1)}, bf16[64,4096]{1,0:T(8,128)(2,1)S(1)}, u32[]{:S(2)}, u32[]{:S(2)}) %collective-permute-start.9) | collective-permute-done | bytes 524320 | tf_op jit(solution)/shard_map/ppermute | solution.py:356
  32.6 2.1 %collective-permute-start.13 = (bf16[64,4096]{1,0:T(8,128)(2,1)S(1)}, bf16[64,4096]{1,0:T(8,128)(2,1)S(1)}, u32[]{:S(2)}, u32[]{:S(2)}) collective-permute-start(bf16[64,4096]{1,0:T(8,128)(2,1)S(1)} %collective-permute-done.9.refs_0_), channel_id=1, source_target_pairs={{0,10},{10,16},{16,26},{26,28},{28,22},{22,12},{12,6},{6,0},{2,4},... | collective-permute-start | bytes 1572872 | tf_op jit(solution)/shard_map/ppermute | solution.py:356
  34.8 0.0 collective-permute-start.6
  34.8 0.0 collective-permute-done.2.refs_3_
  34.8 0.5 collective-permute-start.8
  35.3 0.0 collective-permute-done.4.refs_1_
  35.3 0.1 collective-permute-start.10
  35.3 4.9 %shard_map.37 = (bf16[1024,4096]{1,0:T(8,128)(2,1)S(1)}, f32[8,128]{1,0:T(8,128)S(1)}) custom-call(bf16[1024,4096]{1,0:T(8,128)(2,1)} %grad_ref.1), custom_call_target="tpu_custom_call" | custom-call | flops 8388608 | bytes 8388608 | tf_op jit(solution)/shard_map/pallas_call | solution.py:202
  40.3 0.0 collective-permute-done.11.refs_0_
  40.3 0.5 collective-permute-start.12
  40.8 3.1 %collective-permute-done.13.refs_0_ = bf16[64,4096]{1,0:T(8,128)(2,1)S(1)} collective-permute-done((bf16[64,4096]{1,0:T(8,128)(2,1)S(1)}, bf16[64,4096]{1,0:T(8,128)(2,1)S(1)}, u32[]{:S(2)}, u32[]{:S(2)}) %collective-permute-start.13) | collective-permute-done | bytes 524320 | tf_op jit(solution)/shard_map/ppermute | solution.py:356
  43.9 0.2 collective-permute-start.14
  44.0 0.0 copy-done
  44.0 2.4 %shard_map.38 = (bf16[2,1024,128]{2,1,0:T(8,128)(2,1)S(1)}, bf16[1024,4096]{1,0:T(8,128)(2,1)S(1)}) custom-call(bf16[1024,4096]{1,0:T(8,128)(2,1)S(1)} %get-tuple-element.27.grad_ref, bf16[64,4096]{1,0:T(8,128)(2,1)S(1)} %copy-done, bf16[64,4096]{1,0:T(8,128)(2,1)S(1)} %collective-permute-done.refs_1_, ...), custom_call_target="tpu_custom_call", output_to_operand_aliasing={{1}: (0, {})} | custom-call | flops 2147483648 | bytes 8388608 | tf_op jit(solution)/shard_map/pallas_call | solution.py:155
  46.5 2.4 %shard_map.39 = (bf16[1,1024,128]{2,1,0:T(8,128)(2,1)S(1)}, bf16[1024,4096]{1,0:T(8,128)(2,1)S(1)}) custom-call(bf16[1024,4096]{1,0:T(8,128)(2,1)S(1)} %get-tuple-element.28.grad_ref, bf16[64,4096]{1,0:T(8,128)(2,1)S(1)} %collective-permute-done.3.refs_0_, bf16[64,4096]{1,0:T(8,128)(2,1)S(1)} %collective-permute-done.4.refs_1_), custom_call_target="tpu_custom_call", output_to_operand_aliasing={{1}: (0, {})} | custom-call | flops 1073741824 | bytes 8388608 | tf_op jit(solution)/shard_map/pallas_call | solution.py:155
  48.8 0.0 collective-permute-done.6.refs_1_
  48.8 0.0 collective-permute-done.8.refs_3_
  48.9 2.6 %shard_map.40 = (bf16[2,1024,128]{2,1,0:T(8,128)(2,1)S(1)}, bf16[1024,4096]{1,0:T(8,128)(2,1)S(1)}, bf16[1024,128]{1,0:T(8,128)(2,1)S(1)}) custom-call(bf16[1024,4096]{1,0:T(8,128)(2,1)S(1)} %get-tuple-element.29.grad_ref, bf16[64,4096]{1,0:T(8,128)(2,1)S(1)} %collective-permute-done.5.refs_0_, ...), custom_call_target="tpu_custom_call", output_to_operand_aliasing={{1}: (0, {})} | custom-call | flops 2147483648 | bytes 8388608 | tf_op jit(solution)/shard_map/pallas_call | solution.py:155
  51.4 0.0 collective-permute-done.10.refs_1_
  51.4 2.5 %shard_map.41 = (bf16[1,1024,128]{2,1,0:T(8,128)(2,1)S(1)}, bf16[1024,4096]{1,0:T(8,128)(2,1)S(1)}, bf16[1024,128]{1,0:T(8,128)(2,1)S(1)}) custom-call(bf16[1024,4096]{1,0:T(8,128)(2,1)S(1)} %get-tuple-element.32.grad_ref, bf16[64,4096]{1,0:T(8,128)(2,1)S(1)} %collective-permute-done.9.refs_0_, ...), custom_call_target="tpu_custom_call", output_to_operand_aliasing={{1}: (0, {})} | custom-call | flops 1073741824 | bytes 8388608 | tf_op jit(solution)/shard_map/pallas_call | solution.py:155
  54.0 2.0 %collective-permute-start.17 = (bf16[1024,128]{1,0:T(8,128)(2,1)S(1)}, bf16[1024,128]{1,0:T(8,128)(2,1)S(1)}, u32[]{:S(2)}, u32[]{:S(2)}) collective-permute-start(bf16[1024,128]{1,0:T(8,128)(2,1)S(1)} %get-tuple-element.40), channel_id=1, source_target_pairs={{0,1},{1,0},{2,3},{3,2},{4,5},{5,4},{6,7},{7,6},{8,9},{9,8},{10,11... | collective-permute-start | bytes 786440 | tf_op jit(solution)/shard_map/ppermute | solution.py:352
  56.0 0.1 collective-permute-start.16
  56.1 0.0 collective-permute-done.12.refs_1_
  56.1 2.7 %shard_map.42 = (bf16[1,1024,128]{2,1,0:T(8,128)(2,1)S(1)}, bf16[1024,4096]{1,0:T(8,128)(2,1)S(1)}, bf16[1024,128]{1,0:T(8,128)(2,1)S(1)}) custom-call(bf16[1024,4096]{1,0:T(8,128)(2,1)S(1)} %get-tuple-element.34.grad_ref, bf16[64,4096]{1,0:T(8,128)(2,1)S(1)} %collective-permute-done.11.refs_0_, ...), custom_call_target="tpu_custom_call", output_to_operand_aliasing={{1}: (0, {})} | custom-call | flops 1073741824 | bytes 8388608 | tf_op jit(solution)/shard_map/pallas_call | solution.py:155
  58.8 0.0 copy-start.1
  58.8 2.0 %collective-permute-start.18 = (bf16[1024,128]{1,0:T(8,128)(2,1)S(1)}, bf16[1024,128]{1,0:T(8,128)(2,1)S(1)}, u32[]{:S(2)}, u32[]{:S(2)}) collective-permute-start(bf16[1024,128]{1,0:T(8,128)(2,1)S(1)} %get-tuple-element.41), channel_id=1, source_target_pairs={{0,1},{1,0},{2,3},{3,2},{4,5},{5,4},{6,7},{7,6},{8,9},{9,8},{10,11... | collective-permute-start | bytes 786440 | tf_op jit(solution)/shard_map/ppermute | solution.py:352
  60.8 0.0 collective-permute-done.14.refs_1_
  60.8 2.5 %shard_map.43 = (bf16[1,1024,128]{2,1,0:T(8,128)(2,1)S(1)}, bf16[1024,4096]{1,0:T(8,128)(2,1)S(1)}, bf16[1024,128]{1,0:T(8,128)(2,1)S(1)}) custom-call(bf16[1024,4096]{1,0:T(8,128)(2,1)S(1)} %get-tuple-element.36.grad_ref, bf16[64,4096]{1,0:T(8,128)(2,1)S(1)} %collective-permute-done.13.refs_0_, ...), custom_call_target="tpu_custom_call", output_to_operand_aliasing={{1}: (0, {})} | custom-call | flops 1073741824 | bytes 8388608 | tf_op jit(solution)/shard_map/pallas_call | solution.py:155
  63.3 0.1 collective-permute-start.15
  63.4 1.9 %collective-permute-start.19 = (f32[8,128]{1,0:T(8,128)S(1)}, f32[8,128]{1,0:T(8,128)S(1)}, u32[]{:S(2)}, u32[]{:S(2)}) collective-permute-start(f32[8,128]{1,0:T(8,128)S(1)} %get-tuple-element.42.refs_3_), channel_id=1, source_target_pairs={{0,1},{1,0},{2,3},{3,2},{4,5},{5,4},{6,7},{7,6},{8,9},{9,8},{10,11... | collective-permute-start | bytes 12296 | tf_op jit(solution)/shard_map/ppermute | solution.py:352
  65.4 14.1 %collective-permute-done.19.refs_4_ = f32[8,128]{1,0:T(8,128)S(1)} collective-permute-done((f32[8,128]{1,0:T(8,128)S(1)}, f32[8,128]{1,0:T(8,128)S(1)}, u32[]{:S(2)}, u32[]{:S(2)}) %collective-permute-start.19) | collective-permute-done | bytes 4128 | tf_op jit(solution)/shard_map/ppermute | solution.py:352
  79.5 0.0 collective-permute-done.17.refs_1_
  79.5 0.0 collective-permute-done.16.refs_0_
  79.5 0.0 collective-permute-done.18.refs_2_
  79.5 0.0 copy-done.1
  79.5 1.4 %shard_map.44 = (f32[3,1024,128]{2,1,0:T(8,128)S(1)}, f32[3,2,128]{2,1,0:T(2,128)S(1)}, f32[1024,1]{1,0:T(8,128)S(1)}) custom-call(bf16[1024,128]{1,0:T(8,128)(2,1)S(1)} %collective-permute-done.16.refs_0_, bf16[1024,128]{1,0:T(8,128)(2,1)S(1)} %collective-permute-done.17.refs_1_, bf16[1024,128]{1,0:T(8,128)(2,1)S(1)} %collective-permute-done.18.refs_2_, ...), custom_call_target="tpu_custom_call" | custom-call | flops 3145728 | bytes 4718592 | tf_op jit(solution)/shard_map/pallas_call | solution.py:269
  80.9 0.0 collective-permute-done.15.refs_0_
  81.0 0.4 shard_map.45
  81.4 0.1 collective-permute-start.20
  81.5 1.2 %collective-permute-done.20 = f32[2,512]{1,0:T(2,128)S(1)} collective-permute-done((f32[2,512]{1,0:T(2,128)S(1)}, f32[2,512]{1,0:T(2,128)S(1)}, u32[]{:S(2)}, u32[]{:S(2)}) %collective-permute-start.20) | collective-permute-done | bytes 4128 | tf_op jit(solution)/shard_map/ppermute | solution.py:384
  82.7 1.5 %collective-permute-start.21 = (f32[2,512]{1,0:T(2,128)S(1)}, f32[2,512]{1,0:T(2,128)S(1)}, u32[]{:S(2)}, u32[]{:S(2)}) collective-permute-start(f32[2,512]{1,0:T(2,128)S(1)} %pad_maximum_fusion), channel_id=1, source_target_pairs={{0,6},{2,4},{4,2},{6,0},{8,14},{10,12},{12,10},{14,8},{16,22},{18,... | collective-permute-start | bytes 12296 | tf_op jit(solution)/shard_map/ppermute | solution.py:384
  84.2 1.6 %collective-permute-done.21 = f32[2,512]{1,0:T(2,128)S(1)} collective-permute-done((f32[2,512]{1,0:T(2,128)S(1)}, f32[2,512]{1,0:T(2,128)S(1)}, u32[]{:S(2)}, u32[]{:S(2)}) %collective-permute-start.21) | collective-permute-done | bytes 4128 | tf_op jit(solution)/shard_map/ppermute | solution.py:384
  85.8 1.6 %collective-permute-start.22 = (f32[2,512]{1,0:T(2,128)S(1)}, f32[2,512]{1,0:T(2,128)S(1)}, u32[]{:S(2)}, u32[]{:S(2)}) collective-permute-start(f32[2,512]{1,0:T(2,128)S(1)} %pad_maximum_fusion.1), channel_id=1, source_target_pairs={{0,10},{2,8},{4,14},{6,12},{8,2},{10,0},{12,6},{14,4},{16,26},{18,... | collective-permute-start | bytes 12296 | tf_op jit(solution)/shard_map/ppermute | solution.py:384
  87.4 1.5 %collective-permute-done.22 = f32[2,512]{1,0:T(2,128)S(1)} collective-permute-done((f32[2,512]{1,0:T(2,128)S(1)}, f32[2,512]{1,0:T(2,128)S(1)}, u32[]{:S(2)}, u32[]{:S(2)}) %collective-permute-start.22) | collective-permute-done | bytes 4128 | tf_op jit(solution)/shard_map/ppermute | solution.py:384
  88.9 2.6 %collective-permute-start.23 = (f32[2,512]{1,0:T(2,128)S(1)}, f32[2,512]{1,0:T(2,128)S(1)}, u32[]{:S(2)}, u32[]{:S(2)}) collective-permute-start(f32[2,512]{1,0:T(2,128)S(1)} %pad_maximum_fusion.2), channel_id=1, source_target_pairs={{0,18},{2,16},{4,22},{6,20},{8,26},{10,24},{12,30},{14,28},{16,2},... | collective-permute-start | bytes 12296 | tf_op jit(solution)/shard_map/ppermute | solution.py:384
  91.6 0.4 shard_map.46.scored_ref
  91.9 1.0 %collective-permute-done.23 = f32[2,512]{1,0:T(2,128)S(1)} collective-permute-done((f32[2,512]{1,0:T(2,128)S(1)}, f32[2,512]{1,0:T(2,128)S(1)}, u32[]{:S(2)}, u32[]{:S(2)}) %collective-permute-start.23) | collective-permute-done | bytes 4128 | tf_op jit(solution)/shard_map/ppermute | solution.py:384
  93.0 1.6 %shard_map.47 = bf16[1024,512]{1,0:T(8,128)(2,1)} custom-call(f32[2,512]{1,0:T(2,128)S(1)} %pad_maximum_fusion.3.stat_ref, f32[1024,512]{1,0:T(8,128)S(1)} %shard_map.46.scored_ref), custom_call_target="tpu_custom_call" | custom-call | flops 1048576 | bytes 3145728 | tf_op jit(solution)/shard_map/pallas_call | solution.py:314
  (8 shorter events, 0.1 us)
Async XLA Ops:
  0.0 44.0 %copy-start = (bf16[64,4096]{1,0:T(8,128)(2,1)S(1)}, bf16[64,4096]{1,0:T(8,128)(2,1)}, u32[]{:S(2)}) copy-start(bf16[64,4096]{1,0:T(8,128)(2,1)} %refs_0_.1) | copy-start | bytes 1572868
  0.0 3.2 %collective-permute-start = (bf16[64,4096]{1,0:T(8,128)(2,1)}, bf16[64,4096]{1,0:T(8,128)(2,1)S(1)}, u32[]{:S(2)}, u32[]{:S(2)}) collective-permute-start(bf16[64,4096]{1,0:T(8,128)(2,1)} %refs_0_.1), channel_id=1, source_target_pairs={{0,2},{2,0},{4,6},{6,4},{8,10},{10,8},{12,14},{14,12},{16,18},{18,... | collective-permute-start | bytes 1572872 | tf_op jit(solution)/shard_map/ppermute | solution.py:354
  0.5 9.7 %collective-permute-start.1 = (bf16[64,4096]{1,0:T(8,128)(2,1)}, bf16[64,4096]{1,0:T(8,128)(2,1)S(1)}, u32[]{:S(2)}, u32[]{:S(2)}) collective-permute-start(bf16[64,4096]{1,0:T(8,128)(2,1)} %refs_0_.1), channel_id=1, source_target_pairs={{0,10},{10,16},{16,26},{26,28},{28,22},{22,12},{12,6},{6,0},{2,4},... | collective-permute-start | bytes 1572872 | tf_op jit(solution)/shard_map/ppermute | solution.py:356
  3.2 12.6 %collective-permute-start.3 = (bf16[64,4096]{1,0:T(8,128)(2,1)S(1)}, bf16[64,4096]{1,0:T(8,128)(2,1)S(1)}, u32[]{:S(2)}, u32[]{:S(2)}) collective-permute-start(bf16[64,4096]{1,0:T(8,128)(2,1)S(1)} %collective-permute-done.refs_1_), channel_id=1, source_target_pairs={{0,10},{10,16},{16,26},{26,28},{28,22},{22,12},{12,6},{6,0},{2,4},... | collective-permute-start | bytes 1572872 | tf_op jit(solution)/shard_map/ppermute | solution.py:356
  10.2 11.2 %collective-permute-start.5 = (bf16[64,4096]{1,0:T(8,128)(2,1)S(1)}, bf16[64,4096]{1,0:T(8,128)(2,1)S(1)}, u32[]{:S(2)}, u32[]{:S(2)}) collective-permute-start(bf16[64,4096]{1,0:T(8,128)(2,1)S(1)} %collective-permute-done.1.refs_2_), channel_id=1, source_target_pairs={{0,10},{10,16},{16,26},{26,28},{28,22},{22,12},{12,6},{6,0},{2,4},... | collective-permute-start | bytes 1572872 | tf_op jit(solution)/shard_map/ppermute | solution.py:356
  15.8 11.2 %collective-permute-start.7 = (bf16[64,4096]{1,0:T(8,128)(2,1)S(1)}, bf16[64,4096]{1,0:T(8,128)(2,1)S(1)}, u32[]{:S(2)}, u32[]{:S(2)}) collective-permute-start(bf16[64,4096]{1,0:T(8,128)(2,1)S(1)} %collective-permute-done.3.refs_0_), channel_id=1, source_target_pairs={{0,10},{10,16},{16,26},{26,28},{28,22},{22,12},{12,6},{6,0},{2,4},... | collective-permute-start | bytes 1572872 | tf_op jit(solution)/shard_map/ppermute | solution.py:356
  21.4 11.2 %collective-permute-start.9 = (bf16[64,4096]{1,0:T(8,128)(2,1)S(1)}, bf16[64,4096]{1,0:T(8,128)(2,1)S(1)}, u32[]{:S(2)}, u32[]{:S(2)}) collective-permute-start(bf16[64,4096]{1,0:T(8,128)(2,1)S(1)} %collective-permute-done.5.refs_0_), channel_id=1, source_target_pairs={{0,10},{10,16},{16,26},{26,28},{28,22},{22,12},{12,6},{6,0},{2,4},... | collective-permute-start | bytes 1572872 | tf_op jit(solution)/shard_map/ppermute | solution.py:356
  23.5 11.2 %collective-permute-start.2 = (bf16[64,4096]{1,0:T(8,128)(2,1)S(1)}, bf16[64,4096]{1,0:T(8,128)(2,1)S(1)}, u32[]{:S(2)}, u32[]{:S(2)}) collective-permute-start(bf16[64,4096]{1,0:T(8,128)(2,1)S(1)} %collective-permute-done.1.refs_2_), channel_id=1, source_target_pairs={{0,2},{2,0},{4,6},{6,4},{8,10},{10,8},{12,14},{14,12},{16,18},{18,... | collective-permute-start | bytes 1572872 | tf_op jit(solution)/shard_map/ppermute | solution.py:360
  23.5 11.8 %collective-permute-start.4 = (bf16[64,4096]{1,0:T(8,128)(2,1)S(1)}, bf16[64,4096]{1,0:T(8,128)(2,1)S(1)}, u32[]{:S(2)}, u32[]{:S(2)}) collective-permute-start(bf16[64,4096]{1,0:T(8,128)(2,1)S(1)} %collective-permute-done.3.refs_0_), channel_id=1, source_target_pairs={{0,2},{2,0},{4,6},{6,4},{8,10},{10,8},{12,14},{14,12},{16,18},{18,... | collective-permute-start | bytes 1572872 | tf_op jit(solution)/shard_map/ppermute | solution.py:360
  27.0 13.2 %collective-permute-start.11 = (bf16[64,4096]{1,0:T(8,128)(2,1)S(1)}, bf16[64,4096]{1,0:T(8,128)(2,1)S(1)}, u32[]{:S(2)}, u32[]{:S(2)}) collective-permute-start(bf16[64,4096]{1,0:T(8,128)(2,1)S(1)} %collective-permute-done.7.refs_2_), channel_id=1, source_target_pairs={{0,10},{10,16},{16,26},{26,28},{28,22},{22,12},{12,6},{6,0},{2,4},... | collective-permute-start | bytes 1572872 | tf_op jit(solution)/shard_map/ppermute | solution.py:356
  32.6 11.2 %collective-permute-start.13 = (bf16[64,4096]{1,0:T(8,128)(2,1)S(1)}, bf16[64,4096]{1,0:T(8,128)(2,1)S(1)}, u32[]{:S(2)}, u32[]{:S(2)}) collective-permute-start(bf16[64,4096]{1,0:T(8,128)(2,1)S(1)} %collective-permute-done.9.refs_0_), channel_id=1, source_target_pairs={{0,10},{10,16},{16,26},{26,28},{28,22},{22,12},{12,6},{6,0},{2,4},... | collective-permute-start | bytes 1572872 | tf_op jit(solution)/shard_map/ppermute | solution.py:356
  34.8 14.1 %collective-permute-start.6 = (bf16[64,4096]{1,0:T(8,128)(2,1)S(1)}, bf16[64,4096]{1,0:T(8,128)(2,1)S(1)}, u32[]{:S(2)}, u32[]{:S(2)}) collective-permute-start(bf16[64,4096]{1,0:T(8,128)(2,1)S(1)} %collective-permute-done.5.refs_0_), channel_id=1, source_target_pairs={{0,2},{2,0},{4,6},{6,4},{8,10},{10,8},{12,14},{14,12},{16,18},{18,... | collective-permute-start | bytes 1572872 | tf_op jit(solution)/shard_map/ppermute | solution.py:360
  34.8 14.1 %collective-permute-start.8 = (bf16[64,4096]{1,0:T(8,128)(2,1)S(1)}, bf16[64,4096]{1,0:T(8,128)(2,1)S(1)}, u32[]{:S(2)}, u32[]{:S(2)}) collective-permute-start(bf16[64,4096]{1,0:T(8,128)(2,1)S(1)} %collective-permute-done.7.refs_2_), channel_id=1, source_target_pairs={{0,2},{2,0},{4,6},{6,4},{8,10},{10,8},{12,14},{14,12},{16,18},{18,... | collective-permute-start | bytes 1572872 | tf_op jit(solution)/shard_map/ppermute | solution.py:360
  35.3 16.2 %collective-permute-start.10 = (bf16[64,4096]{1,0:T(8,128)(2,1)S(1)}, bf16[64,4096]{1,0:T(8,128)(2,1)S(1)}, u32[]{:S(2)}, u32[]{:S(2)}) collective-permute-start(bf16[64,4096]{1,0:T(8,128)(2,1)S(1)} %collective-permute-done.9.refs_0_), channel_id=1, source_target_pairs={{0,2},{2,0},{4,6},{6,4},{8,10},{10,8},{12,14},{14,12},{16,18},{18,... | collective-permute-start | bytes 1572872 | tf_op jit(solution)/shard_map/ppermute | solution.py:360
  40.3 15.8 %collective-permute-start.12 = (bf16[64,4096]{1,0:T(8,128)(2,1)S(1)}, bf16[64,4096]{1,0:T(8,128)(2,1)S(1)}, u32[]{:S(2)}, u32[]{:S(2)}) collective-permute-start(bf16[64,4096]{1,0:T(8,128)(2,1)S(1)} %collective-permute-done.11.refs_0_), channel_id=1, source_target_pairs={{0,2},{2,0},{4,6},{6,4},{8,10},{10,8},{12,14},{14,12},{16,18},{18,... | collective-permute-start | bytes 1572872 | tf_op jit(solution)/shard_map/ppermute | solution.py:360
  43.9 16.9 %collective-permute-start.14 = (bf16[64,4096]{1,0:T(8,128)(2,1)S(1)}, bf16[64,4096]{1,0:T(8,128)(2,1)S(1)}, u32[]{:S(2)}, u32[]{:S(2)}) collective-permute-start(bf16[64,4096]{1,0:T(8,128)(2,1)S(1)} %collective-permute-done.13.refs_0_), channel_id=1, source_target_pairs={{0,2},{2,0},{4,6},{6,4},{8,10},{10,8},{12,14},{14,12},{16,18},{18,... | collective-permute-start | bytes 1572872 | tf_op jit(solution)/shard_map/ppermute | solution.py:360
  54.0 25.6 %collective-permute-start.17 = (bf16[1024,128]{1,0:T(8,128)(2,1)S(1)}, bf16[1024,128]{1,0:T(8,128)(2,1)S(1)}, u32[]{:S(2)}, u32[]{:S(2)}) collective-permute-start(bf16[1024,128]{1,0:T(8,128)(2,1)S(1)} %get-tuple-element.40), channel_id=1, source_target_pairs={{0,1},{1,0},{2,3},{3,2},{4,5},{5,4},{6,7},{7,6},{8,9},{9,8},{10,11... | collective-permute-start | bytes 786440 | tf_op jit(solution)/shard_map/ppermute | solution.py:352
  56.0 23.5 %collective-permute-start.16 = (bf16[1024,128]{1,0:T(8,128)(2,1)S(1)}, bf16[1024,128]{1,0:T(8,128)(2,1)S(1)}, u32[]{:S(2)}, u32[]{:S(2)}) collective-permute-start(bf16[1024,128]{1,0:T(8,128)(2,1)S(1)} %get-tuple-element.39), channel_id=1, source_target_pairs={{0,1},{1,0},{2,3},{3,2},{4,5},{5,4},{6,7},{7,6},{8,9},{9,8},{10,11... | collective-permute-start | bytes 786440 | tf_op jit(solution)/shard_map/ppermute | solution.py:352
  58.8 20.8 %copy-start.1 = (f32[1024]{0:T(1024)S(1)}, f32[1024]{0:T(1024)}, u32[]{:S(2)}) copy-start(f32[1024]{0:T(1024)} %param.5) | copy-start | bytes 12292
  58.8 20.8 %collective-permute-start.18 = (bf16[1024,128]{1,0:T(8,128)(2,1)S(1)}, bf16[1024,128]{1,0:T(8,128)(2,1)S(1)}, u32[]{:S(2)}, u32[]{:S(2)}) collective-permute-start(bf16[1024,128]{1,0:T(8,128)(2,1)S(1)} %get-tuple-element.41), channel_id=1, source_target_pairs={{0,1},{1,0},{2,3},{3,2},{4,5},{5,4},{6,7},{7,6},{8,9},{9,8},{10,11... | collective-permute-start | bytes 786440 | tf_op jit(solution)/shard_map/ppermute | solution.py:352
  63.3 17.7 %collective-permute-start.15 = (bf16[1024,128]{1,0:T(8,128)(2,1)S(1)}, bf16[1024,128]{1,0:T(8,128)(2,1)S(1)}, u32[]{:S(2)}, u32[]{:S(2)}) collective-permute-start(bf16[1024,128]{1,0:T(8,128)(2,1)S(1)} %get-tuple-element.38), channel_id=1, source_target_pairs={{0,1},{1,0},{2,3},{3,2},{4,5},{5,4},{6,7},{7,6},{8,9},{9,8},{10,11... | collective-permute-start | bytes 786440 | tf_op jit(solution)/shard_map/ppermute | solution.py:352
  63.4 16.1 %collective-permute-start.19 = (f32[8,128]{1,0:T(8,128)S(1)}, f32[8,128]{1,0:T(8,128)S(1)}, u32[]{:S(2)}, u32[]{:S(2)}) collective-permute-start(f32[8,128]{1,0:T(8,128)S(1)} %get-tuple-element.42.refs_3_), channel_id=1, source_target_pairs={{0,1},{1,0},{2,3},{3,2},{4,5},{5,4},{6,7},{7,6},{8,9},{9,8},{10,11... | collective-permute-start | bytes 12296 | tf_op jit(solution)/shard_map/ppermute | solution.py:352
  81.4 1.2 %collective-permute-start.20 = (f32[2,512]{1,0:T(2,128)S(1)}, f32[2,512]{1,0:T(2,128)S(1)}, u32[]{:S(2)}, u32[]{:S(2)}) collective-permute-start(f32[2,512]{1,0:T(2,128)S(1)} %get-tuple-element.46), channel_id=1, source_target_pairs={{0,2},{2,0},{4,6},{6,4},{8,10},{10,8},{12,14},{14,12},{16,18},{18,... | collective-permute-start | bytes 12296 | tf_op jit(solution)/shard_map/ppermute | solution.py:384
  82.7 3.1 %collective-permute-start.21 = (f32[2,512]{1,0:T(2,128)S(1)}, f32[2,512]{1,0:T(2,128)S(1)}, u32[]{:S(2)}, u32[]{:S(2)}) collective-permute-start(f32[2,512]{1,0:T(2,128)S(1)} %pad_maximum_fusion), channel_id=1, source_target_pairs={{0,6},{2,4},{4,2},{6,0},{8,14},{10,12},{12,10},{14,8},{16,22},{18,... | collective-permute-start | bytes 12296 | tf_op jit(solution)/shard_map/ppermute | solution.py:384
  85.8 3.1 %collective-permute-start.22 = (f32[2,512]{1,0:T(2,128)S(1)}, f32[2,512]{1,0:T(2,128)S(1)}, u32[]{:S(2)}, u32[]{:S(2)}) collective-permute-start(f32[2,512]{1,0:T(2,128)S(1)} %pad_maximum_fusion.1), channel_id=1, source_target_pairs={{0,10},{2,8},{4,14},{6,12},{8,2},{10,0},{12,6},{14,4},{16,26},{18,... | collective-permute-start | bytes 12296 | tf_op jit(solution)/shard_map/ppermute | solution.py:384
  88.9 4.0 %collective-permute-start.23 = (f32[2,512]{1,0:T(2,128)S(1)}, f32[2,512]{1,0:T(2,128)S(1)}, u32[]{:S(2)}, u32[]{:S(2)}) collective-permute-start(f32[2,512]{1,0:T(2,128)S(1)} %pad_maximum_fusion.2), channel_id=1, source_target_pairs={{0,18},{2,16},{4,22},{6,20},{8,26},{10,24},{12,30},{14,28},{16,2},... | collective-permute-start | bytes 12296 | tf_op jit(solution)/shard_map/ppermute | solution.py:384

commit v3 on v2

--- a/solution.py
+++ b/solution.py
@@ -197,7 +197,7 @@
         square_ref[i:i + 1, :] = jnp.sum(jnp.where(diagonal(), column, 0.0), axis=0, keepdims=True)
 
 
-def load_call(gradients, parts=4):
+def load_call(gradients, parts=8):
     rows, depth = gradients.shape
     return pl.pallas_call(
         functools.partial(load_kernel, parts),
@@ -302,21 +302,30 @@
     )(early, late)
 
 
-def finish_kernel(count, stat_ref, scored_ref, out_ref):
-    rows = out_ref.shape[0]
-    here = pl.ds(pl.multiple_of(pl.program_id(0) * rows, rows), rows)
+def finish_kernel(count, stat_ref, scored_ref, out_ref, held, sem):
     scale = lax.rsqrt(stat_ref[1:2, :] / count + VAR_EPS)
-    out_ref[...] = ((scored_ref[here, :] - stat_ref[0:1, :]) * scale).astype(jnp.bfloat16)
-
-
-def finish_call(count, stat, scored, steps=4):
+    steps, rows = held.shape[0], held.shape[1]
+    copies = []
+    for i in range(steps):
+        here = slice(i * rows, (i + 1) * rows)
+        held[i] = ((scored_ref[here, :] - stat_ref[0:1, :]) * scale).astype(jnp.bfloat16)
+        copies.append(pltpu.make_async_copy(held.at[i], out_ref.at[pl.ds(i * rows, rows)], sem.at[i]))
+        copies[i].start()
+    for copy in copies:
+        copy.wait()
+
+
+def finish_call(count, stat, scored, steps=8):
     rows, width = scored.shape
     return pl.pallas_call(
         functools.partial(finish_kernel, count),
-        grid=(steps,),
         out_shape=jax.ShapeDtypeStruct((rows, width), jnp.bfloat16),
         in_specs=[VMEM] * 2,
-        out_specs=pl.BlockSpec((rows // steps, width), lambda i: (i, 0)),
+        out_specs=pl.BlockSpec(memory_space=pltpu.HBM),
+        scratch_shapes=[
+            pltpu.VMEM((steps, rows // steps, width), jnp.bfloat16),
+            pltpu.SemaphoreType.DMA((steps,)),
+        ],
         compiler_params=pltpu.CompilerParams(vmem_limit_bytes=8 * 1024 * 1024),
         cost_estimate=pl.CostEstimate(flops=2 * rows * width, bytes_accessed=6 * rows * width, transcendentals=0),
     )(stat, scored)

time: 94.7 us -> 94.5 us (level)
  no operation moved by 1% of the time
where the time goes in v3:
time: 94.5 us; the launch traced here: 94.4 us
  waiting for transfers between devices  41.7 us (44%)
  starting transfers between devices  29.3 us (31%)
  Pallas kernels  22.9 us (24%)
    ppermute x7, waiting for transfers between devices, ring_body(): ring.append(lax.ppermute(ring[-2], 'rows', turn))  22.2 us
    pallas_call x6, Pallas kernels, product_call(): pl.pallas_call(functools.partial(product_kernel, plan, sources, count, tu...  15 us
    ppermute x7, starting transfers between devices, ring_body(): ring.append(lax.ppermute(ring[-2], 'rows', turn))  15 us
    ppermute x5, waiting for transfers between devices, cross(): return lax.ppermute(value, 'feat', [(0, 1), (1, 0)])  14.3 us
    ppermute x5, starting transfers between devices, cross(): return lax.ppermute(value, 'feat', [(0, 1), (1, 0)])  6.21 us
    ppermute x4, starting transfers between devices, ring_body(): come = lax.ppermute(jnp.concatenate([mean, spread], axis=0), 'rows', pairs)  5.85 us
    ppermute x4, waiting for transfers between devices, ring_body(): come = lax.ppermute(jnp.concatenate([mean, spread], axis=0), 'rows', pairs)  5.19 us
    pallas_call x1, Pallas kernels, load_call(): pl.pallas_call(functools.partial(load_kernel, parts), out_shape=[jax.Shap...  4.58 us
  transfers between devices with their start and end apart: 24, of which 11 were waited for; matrix products, arithmetic and copies ran while one was open for 0% of the time, Pallas kernels for 23%

profile of v3, /device:TPU:0, one launch (start us, length us, event | category | flops | bytes accessed | tf_op | source)
XLA Modules:
  0.0 94.4 jit_solution(10955263785788353365)
XLA Ops:
  0.0 0.0 copy-start
  0.0 0.5 collective-permute-start
  0.5 2.7 %collective-permute-start.1 = (bf16[64,4096]{1,0:T(8,128)(2,1)}, bf16[64,4096]{1,0:T(8,128)(2,1)S(1)}, u32[]{:S(2)}, u32[]{:S(2)}) collective-permute-start(bf16[64,4096]{1,0:T(8,128)(2,1)} %refs_0_.1), channel_id=1, source_target_pairs={{0,10},{10,16},{16,26},{26,28},{28,22},{22,12},{12,6},{6,0},{2,4},... | collective-permute-start | bytes 1572872 | tf_op jit(solution)/shard_map/ppermute | solution.py:365
  3.2 0.0 collective-permute-done.refs_1_
  3.2 1.7 %collective-permute-start.3 = (bf16[64,4096]{1,0:T(8,128)(2,1)S(1)}, bf16[64,4096]{1,0:T(8,128)(2,1)S(1)}, u32[]{:S(2)}, u32[]{:S(2)}) collective-permute-start(bf16[64,4096]{1,0:T(8,128)(2,1)S(1)} %collective-permute-done.refs_1_), channel_id=1, source_target_pairs={{0,10},{10,16},{16,26},{26,28},{28,22},{22,12},{12,6},{6,0},{2,4},... | collective-permute-start | bytes 1572872 | tf_op jit(solution)/shard_map/ppermute | solution.py:365
  4.9 5.3 %collective-permute-done.1.refs_2_ = bf16[64,4096]{1,0:T(8,128)(2,1)S(1)} collective-permute-done((bf16[64,4096]{1,0:T(8,128)(2,1)}, bf16[64,4096]{1,0:T(8,128)(2,1)S(1)}, u32[]{:S(2)}, u32[]{:S(2)}) %collective-permute-start.1) | collective-permute-done | bytes 524320 | tf_op jit(solution)/shard_map/ppermute | solution.py:365
  10.2 2.1 %collective-permute-start.5 = (bf16[64,4096]{1,0:T(8,128)(2,1)S(1)}, bf16[64,4096]{1,0:T(8,128)(2,1)S(1)}, u32[]{:S(2)}, u32[]{:S(2)}) collective-permute-start(bf16[64,4096]{1,0:T(8,128)(2,1)S(1)} %collective-permute-done.1.refs_2_), channel_id=1, source_target_pairs={{0,10},{10,16},{16,26},{26,28},{28,22},{22,12},{12,6},{6,0},{2,4},... | collective-permute-start | bytes 1572872 | tf_op jit(solution)/shard_map/ppermute | solution.py:365
  12.3 3.5 %collective-permute-done.3.refs_0_ = bf16[64,4096]{1,0:T(8,128)(2,1)S(1)} collective-permute-done((bf16[64,4096]{1,0:T(8,128)(2,1)S(1)}, bf16[64,4096]{1,0:T(8,128)(2,1)S(1)}, u32[]{:S(2)}, u32[]{:S(2)}) %collective-permute-start.3) | collective-permute-done | bytes 524320 | tf_op jit(solution)/shard_map/ppermute | solution.py:365
  15.8 2.1 %collective-permute-start.7 = (bf16[64,4096]{1,0:T(8,128)(2,1)S(1)}, bf16[64,4096]{1,0:T(8,128)(2,1)S(1)}, u32[]{:S(2)}, u32[]{:S(2)}) collective-permute-start(bf16[64,4096]{1,0:T(8,128)(2,1)S(1)} %collective-permute-done.3.refs_0_), channel_id=1, source_target_pairs={{0,10},{10,16},{16,26},{26,28},{28,22},{22,12},{12,6},{6,0},{2,4},... | collective-permute-start | bytes 1572872 | tf_op jit(solution)/shard_map/ppermute | solution.py:365
  17.9 3.5 %collective-permute-done.5.refs_0_ = bf16[64,4096]{1,0:T(8,128)(2,1)S(1)} collective-permute-done((bf16[64,4096]{1,0:T(8,128)(2,1)S(1)}, bf16[64,4096]{1,0:T(8,128)(2,1)S(1)}, u32[]{:S(2)}, u32[]{:S(2)}) %collective-permute-start.5) | collective-permute-done | bytes 524320 | tf_op jit(solution)/shard_map/ppermute | solution.py:365
  21.4 2.1 %collective-permute-start.9 = (bf16[64,4096]{1,0:T(8,128)(2,1)S(1)}, bf16[64,4096]{1,0:T(8,128)(2,1)S(1)}, u32[]{:S(2)}, u32[]{:S(2)}) collective-permute-start(bf16[64,4096]{1,0:T(8,128)(2,1)S(1)} %collective-permute-done.5.refs_0_), channel_id=1, source_target_pairs={{0,10},{10,16},{16,26},{26,28},{28,22},{22,12},{12,6},{6,0},{2,4},... | collective-permute-start | bytes 1572872 | tf_op jit(solution)/shard_map/ppermute | solution.py:365
  23.5 0.0 collective-permute-start.2
  23.5 0.5 collective-permute-start.4
  24.0 3.0 %collective-permute-done.7.refs_2_ = bf16[64,4096]{1,0:T(8,128)(2,1)S(1)} collective-permute-done((bf16[64,4096]{1,0:T(8,128)(2,1)S(1)}, bf16[64,4096]{1,0:T(8,128)(2,1)S(1)}, u32[]{:S(2)}, u32[]{:S(2)}) %collective-permute-start.7) | collective-permute-done | bytes 524320 | tf_op jit(solution)/shard_map/ppermute | solution.py:365
  27.0 2.1 %collective-permute-start.11 = (bf16[64,4096]{1,0:T(8,128)(2,1)S(1)}, bf16[64,4096]{1,0:T(8,128)(2,1)S(1)}, u32[]{:S(2)}, u32[]{:S(2)}) collective-permute-start(bf16[64,4096]{1,0:T(8,128)(2,1)S(1)} %collective-permute-done.7.refs_2_), channel_id=1, source_target_pairs={{0,10},{10,16},{16,26},{26,28},{28,22},{22,12},{12,6},{6,0},{2,4},... | collective-permute-start | bytes 1572872 | tf_op jit(solution)/shard_map/ppermute | solution.py:365
  29.1 3.5 %collective-permute-done.9.refs_0_ = bf16[64,4096]{1,0:T(8,128)(2,1)S(1)} collective-permute-done((bf16[64,4096]{1,0:T(8,128)(2,1)S(1)}, bf16[64,4096]{1,0:T(8,128)(2,1)S(1)}, u32[]{:S(2)}, u32[]{:S(2)}) %collective-permute-start.9) | collective-permute-done | bytes 524320 | tf_op jit(solution)/shard_map/ppermute | solution.py:365
  32.6 2.1 %collective-permute-start.13 = (bf16[64,4096]{1,0:T(8,128)(2,1)S(1)}, bf16[64,4096]{1,0:T(8,128)(2,1)S(1)}, u32[]{:S(2)}, u32[]{:S(2)}) collective-permute-start(bf16[64,4096]{1,0:T(8,128)(2,1)S(1)} %collective-permute-done.9.refs_0_), channel_id=1, source_target_pairs={{0,10},{10,16},{16,26},{26,28},{28,22},{22,12},{12,6},{6,0},{2,4},... | collective-permute-start | bytes 1572872 | tf_op jit(solution)/shard_map/ppermute | solution.py:365
  34.8 0.0 collective-permute-start.6
  34.8 0.0 collective-permute-done.2.refs_3_
  34.8 0.5 collective-permute-start.8
  35.3 0.0 collective-permute-done.4.refs_1_
  35.3 0.1 collective-permute-start.10
  35.3 4.6 %shard_map.37 = (bf16[1024,4096]{1,0:T(8,128)(2,1)S(1)}, f32[8,128]{1,0:T(8,128)S(1)}) custom-call(bf16[1024,4096]{1,0:T(8,128)(2,1)} %grad_ref.1), custom_call_target="tpu_custom_call" | custom-call | flops 8388608 | bytes 8388608 | tf_op jit(solution)/shard_map/pallas_call | solution.py:202
  39.9 0.0 collective-permute-done.11.refs_0_
  39.9 0.5 collective-permute-start.12
  40.4 3.4 %collective-permute-done.13.refs_0_ = bf16[64,4096]{1,0:T(8,128)(2,1)S(1)} collective-permute-done((bf16[64,4096]{1,0:T(8,128)(2,1)S(1)}, bf16[64,4096]{1,0:T(8,128)(2,1)S(1)}, u32[]{:S(2)}, u32[]{:S(2)}) %collective-permute-start.13) | collective-permute-done | bytes 524320 | tf_op jit(solution)/shard_map/ppermute | solution.py:365
  43.9 0.2 collective-permute-start.14
  44.0 0.0 copy-done
  44.0 2.4 %shard_map.38 = (bf16[2,1024,128]{2,1,0:T(8,128)(2,1)S(1)}, bf16[1024,4096]{1,0:T(8,128)(2,1)S(1)}) custom-call(bf16[1024,4096]{1,0:T(8,128)(2,1)S(1)} %get-tuple-element.27.grad_ref, bf16[64,4096]{1,0:T(8,128)(2,1)S(1)} %copy-done, bf16[64,4096]{1,0:T(8,128)(2,1)S(1)} %collective-permute-done.refs_1_, ...), custom_call_target="tpu_custom_call", output_to_operand_aliasing={{1}: (0, {})} | custom-call | flops 2147483648 | bytes 8388608 | tf_op jit(solution)/shard_map/pallas_call | solution.py:155
  46.5 2.4 %shard_map.39 = (bf16[1,1024,128]{2,1,0:T(8,128)(2,1)S(1)}, bf16[1024,4096]{1,0:T(8,128)(2,1)S(1)}) custom-call(bf16[1024,4096]{1,0:T(8,128)(2,1)S(1)} %get-tuple-element.28.grad_ref, bf16[64,4096]{1,0:T(8,128)(2,1)S(1)} %collective-permute-done.3.refs_0_, bf16[64,4096]{1,0:T(8,128)(2,1)S(1)} %collective-permute-done.4.refs_1_), custom_call_target="tpu_custom_call", output_to_operand_aliasing={{1}: (0, {})} | custom-call | flops 1073741824 | bytes 8388608 | tf_op jit(solution)/shard_map/pallas_call | solution.py:155
  48.8 0.0 collective-permute-done.6.refs_1_
  48.8 0.0 collective-permute-done.8.refs_3_
  48.9 2.6 %shard_map.40 = (bf16[2,1024,128]{2,1,0:T(8,128)(2,1)S(1)}, bf16[1024,4096]{1,0:T(8,128)(2,1)S(1)}, bf16[1024,128]{1,0:T(8,128)(2,1)S(1)}) custom-call(bf16[1024,4096]{1,0:T(8,128)(2,1)S(1)} %get-tuple-element.29.grad_ref, bf16[64,4096]{1,0:T(8,128)(2,1)S(1)} %collective-permute-done.5.refs_0_, ...), custom_call_target="tpu_custom_call", output_to_operand_aliasing={{1}: (0, {})} | custom-call | flops 2147483648 | bytes 8388608 | tf_op jit(solution)/shard_map/pallas_call | solution.py:155
  51.4 0.0 collective-permute-done.10.refs_1_
  51.4 2.7 %shard_map.41 = (bf16[1,1024,128]{2,1,0:T(8,128)(2,1)S(1)}, bf16[1024,4096]{1,0:T(8,128)(2,1)S(1)}, bf16[1024,128]{1,0:T(8,128)(2,1)S(1)}) custom-call(bf16[1024,4096]{1,0:T(8,128)(2,1)S(1)} %get-tuple-element.32.grad_ref, bf16[64,4096]{1,0:T(8,128)(2,1)S(1)} %collective-permute-done.9.refs_0_, ...), custom_call_target="tpu_custom_call", output_to_operand_aliasing={{1}: (0, {})} | custom-call | flops 1073741824 | bytes 8388608 | tf_op jit(solution)/shard_map/pallas_call | solution.py:155
  54.1 2.0 %collective-permute-start.17 = (bf16[1024,128]{1,0:T(8,128)(2,1)S(1)}, bf16[1024,128]{1,0:T(8,128)(2,1)S(1)}, u32[]{:S(2)}, u32[]{:S(2)}) collective-permute-start(bf16[1024,128]{1,0:T(8,128)(2,1)S(1)} %get-tuple-element.40), channel_id=1, source_target_pairs={{0,1},{1,0},{2,3},{3,2},{4,5},{5,4},{6,7},{7,6},{8,9},{9,8},{10,11... | collective-permute-start | bytes 786440 | tf_op jit(solution)/shard_map/ppermute | solution.py:361
  56.2 0.1 collective-permute-start.16
  56.3 0.0 collective-permute-done.12.refs_1_
  56.3 2.5 %shard_map.42 = (bf16[1,1024,128]{2,1,0:T(8,128)(2,1)S(1)}, bf16[1024,4096]{1,0:T(8,128)(2,1)S(1)}, bf16[1024,128]{1,0:T(8,128)(2,1)S(1)}) custom-call(bf16[1024,4096]{1,0:T(8,128)(2,1)S(1)} %get-tuple-element.34.grad_ref, bf16[64,4096]{1,0:T(8,128)(2,1)S(1)} %collective-permute-done.11.refs_0_, ...), custom_call_target="tpu_custom_call", output_to_operand_aliasing={{1}: (0, {})} | custom-call | flops 1073741824 | bytes 8388608 | tf_op jit(solution)/shard_map/pallas_call | solution.py:155
  58.8 0.0 copy-start.1
  58.8 2.0 %collective-permute-start.18 = (bf16[1024,128]{1,0:T(8,128)(2,1)S(1)}, bf16[1024,128]{1,0:T(8,128)(2,1)S(1)}, u32[]{:S(2)}, u32[]{:S(2)}) collective-permute-start(bf16[1024,128]{1,0:T(8,128)(2,1)S(1)} %get-tuple-element.41), channel_id=1, source_target_pairs={{0,1},{1,0},{2,3},{3,2},{4,5},{5,4},{6,7},{7,6},{8,9},{9,8},{10,11... | collective-permute-start | bytes 786440 | tf_op jit(solution)/shard_map/ppermute | solution.py:361
  60.8 0.0 collective-permute-done.14.refs_1_
  60.8 2.5 %shard_map.43 = (bf16[1,1024,128]{2,1,0:T(8,128)(2,1)S(1)}, bf16[1024,4096]{1,0:T(8,128)(2,1)S(1)}, bf16[1024,128]{1,0:T(8,128)(2,1)S(1)}) custom-call(bf16[1024,4096]{1,0:T(8,128)(2,1)S(1)} %get-tuple-element.36.grad_ref, bf16[64,4096]{1,0:T(8,128)(2,1)S(1)} %collective-permute-done.13.refs_0_, ...), custom_call_target="tpu_custom_call", output_to_operand_aliasing={{1}: (0, {})} | custom-call | flops 1073741824 | bytes 8388608 | tf_op jit(solution)/shard_map/pallas_call | solution.py:155
  63.3 0.1 collective-permute-start.15
  63.4 2.0 %collective-permute-start.19 = (f32[8,128]{1,0:T(8,128)S(1)}, f32[8,128]{1,0:T(8,128)S(1)}, u32[]{:S(2)}, u32[]{:S(2)}) collective-permute-start(f32[8,128]{1,0:T(8,128)S(1)} %get-tuple-element.42.refs_3_), channel_id=1, source_target_pairs={{0,1},{1,0},{2,3},{3,2},{4,5},{5,4},{6,7},{7,6},{8,9},{9,8},{10,11... | collective-permute-start | bytes 12296 | tf_op jit(solution)/shard_map/ppermute | solution.py:361
  65.4 14.3 %collective-permute-done.19.refs_4_ = f32[8,128]{1,0:T(8,128)S(1)} collective-permute-done((f32[8,128]{1,0:T(8,128)S(1)}, f32[8,128]{1,0:T(8,128)S(1)}, u32[]{:S(2)}, u32[]{:S(2)}) %collective-permute-start.19) | collective-permute-done | bytes 4128 | tf_op jit(solution)/shard_map/ppermute | solution.py:361
  79.7 0.0 collective-permute-done.17.refs_1_
  79.7 0.0 collective-permute-done.16.refs_0_
  79.7 0.0 collective-permute-done.18.refs_2_
  79.7 0.0 copy-done.1
  79.7 1.4 %shard_map.44 = (f32[3,1024,128]{2,1,0:T(8,128)S(1)}, f32[3,2,128]{2,1,0:T(2,128)S(1)}, f32[1024,1]{1,0:T(8,128)S(1)}) custom-call(bf16[1024,128]{1,0:T(8,128)(2,1)S(1)} %collective-permute-done.16.refs_0_, bf16[1024,128]{1,0:T(8,128)(2,1)S(1)} %collective-permute-done.17.refs_1_, bf16[1024,128]{1,0:T(8,128)(2,1)S(1)} %collective-permute-done.18.refs_2_, ...), custom_call_target="tpu_custom_call" | custom-call | flops 3145728 | bytes 4718592 | tf_op jit(solution)/shard_map/pallas_call | solution.py:269
  81.1 0.0 collective-permute-done.15.refs_0_
  81.1 0.4 shard_map.45
  81.6 0.1 collective-permute-start.20
  81.7 1.2 %collective-permute-done.20 = f32[2,512]{1,0:T(2,128)S(1)} collective-permute-done((f32[2,512]{1,0:T(2,128)S(1)}, f32[2,512]{1,0:T(2,128)S(1)}, u32[]{:S(2)}, u32[]{:S(2)}) %collective-permute-start.20) | collective-permute-done | bytes 4128 | tf_op jit(solution)/shard_map/ppermute | solution.py:393
  82.9 1.5 %collective-permute-start.21 = (f32[2,512]{1,0:T(2,128)S(1)}, f32[2,512]{1,0:T(2,128)S(1)}, u32[]{:S(2)}, u32[]{:S(2)}) collective-permute-start(f32[2,512]{1,0:T(2,128)S(1)} %pad_maximum_fusion), channel_id=1, source_target_pairs={{0,6},{2,4},{4,2},{6,0},{8,14},{10,12},{12,10},{14,8},{16,22},{18,... | collective-permute-start | bytes 12296 | tf_op jit(solution)/shard_map/ppermute | solution.py:393
  84.4 1.6 %collective-permute-done.21 = f32[2,512]{1,0:T(2,128)S(1)} collective-permute-done((f32[2,512]{1,0:T(2,128)S(1)}, f32[2,512]{1,0:T(2,128)S(1)}, u32[]{:S(2)}, u32[]{:S(2)}) %collective-permute-start.21) | collective-permute-done | bytes 4128 | tf_op jit(solution)/shard_map/ppermute | solution.py:393
  86.0 1.6 %collective-permute-start.22 = (f32[2,512]{1,0:T(2,128)S(1)}, f32[2,512]{1,0:T(2,128)S(1)}, u32[]{:S(2)}, u32[]{:S(2)}) collective-permute-start(f32[2,512]{1,0:T(2,128)S(1)} %pad_maximum_fusion.1), channel_id=1, source_target_pairs={{0,10},{2,8},{4,14},{6,12},{8,2},{10,0},{12,6},{14,4},{16,26},{18,... | collective-permute-start | bytes 12296 | tf_op jit(solution)/shard_map/ppermute | solution.py:393
  87.6 1.5 %collective-permute-done.22 = f32[2,512]{1,0:T(2,128)S(1)} collective-permute-done((f32[2,512]{1,0:T(2,128)S(1)}, f32[2,512]{1,0:T(2,128)S(1)}, u32[]{:S(2)}, u32[]{:S(2)}) %collective-permute-start.22) | collective-permute-done | bytes 4128 | tf_op jit(solution)/shard_map/ppermute | solution.py:393
  89.1 2.6 %collective-permute-start.23 = (f32[2,512]{1,0:T(2,128)S(1)}, f32[2,512]{1,0:T(2,128)S(1)}, u32[]{:S(2)}, u32[]{:S(2)}) collective-permute-start(f32[2,512]{1,0:T(2,128)S(1)} %pad_maximum_fusion.2), channel_id=1, source_target_pairs={{0,18},{2,16},{4,22},{6,20},{8,26},{10,24},{12,30},{14,28},{16,2},... | collective-permute-start | bytes 12296 | tf_op jit(solution)/shard_map/ppermute | solution.py:393
  91.7 0.4 shard_map.46.scored_ref
  92.1 1.0 %collective-permute-done.23 = f32[2,512]{1,0:T(2,128)S(1)} collective-permute-done((f32[2,512]{1,0:T(2,128)S(1)}, f32[2,512]{1,0:T(2,128)S(1)}, u32[]{:S(2)}, u32[]{:S(2)}) %collective-permute-start.23) | collective-permute-done | bytes 4128 | tf_op jit(solution)/shard_map/ppermute | solution.py:393
  93.1 1.1 %shard_map.47 = bf16[1024,512]{1,0:T(8,128)(2,1)} custom-call(f32[2,512]{1,0:T(2,128)S(1)} %pad_maximum_fusion.3.stat_ref, f32[1024,512]{1,0:T(8,128)S(1)} %shard_map.46.scored_ref), custom_call_target="tpu_custom_call" | custom-call | flops 1048576 | bytes 3145728 | tf_op jit(solution)/shard_map/pallas_call | solution.py:320
  (8 shorter events, 0.1 us)
Async XLA Ops:
  0.0 44.0 %copy-start = (bf16[64,4096]{1,0:T(8,128)(2,1)S(1)}, bf16[64,4096]{1,0:T(8,128)(2,1)}, u32[]{:S(2)}) copy-start(bf16[64,4096]{1,0:T(8,128)(2,1)} %refs_0_.1) | copy-start | bytes 1572868
  0.0 3.2 %collective-permute-start = (bf16[64,4096]{1,0:T(8,128)(2,1)}, bf16[64,4096]{1,0:T(8,128)(2,1)S(1)}, u32[]{:S(2)}, u32[]{:S(2)}) collective-permute-start(bf16[64,4096]{1,0:T(8,128)(2,1)} %refs_0_.1), channel_id=1, source_target_pairs={{0,2},{2,0},{4,6},{6,4},{8,10},{10,8},{12,14},{14,12},{16,18},{18,... | collective-permute-start | bytes 1572872 | tf_op jit(solution)/shard_map/ppermute | solution.py:363
  0.5 9.7 %collective-permute-start.1 = (bf16[64,4096]{1,0:T(8,128)(2,1)}, bf16[64,4096]{1,0:T(8,128)(2,1)S(1)}, u32[]{:S(2)}, u32[]{:S(2)}) collective-permute-start(bf16[64,4096]{1,0:T(8,128)(2,1)} %refs_0_.1), channel_id=1, source_target_pairs={{0,10},{10,16},{16,26},{26,28},{28,22},{22,12},{12,6},{6,0},{2,4},... | collective-permute-start | bytes 1572872 | tf_op jit(solution)/shard_map/ppermute | solution.py:365
  3.2 12.6 %collective-permute-start.3 = (bf16[64,4096]{1,0:T(8,128)(2,1)S(1)}, bf16[64,4096]{1,0:T(8,128)(2,1)S(1)}, u32[]{:S(2)}, u32[]{:S(2)}) collective-permute-start(bf16[64,4096]{1,0:T(8,128)(2,1)S(1)} %collective-permute-done.refs_1_), channel_id=1, source_target_pairs={{0,10},{10,16},{16,26},{26,28},{28,22},{22,12},{12,6},{6,0},{2,4},... | collective-permute-start | bytes 1572872 | tf_op jit(solution)/shard_map/ppermute | solution.py:365
  10.2 11.2 %collective-permute-start.5 = (bf16[64,4096]{1,0:T(8,128)(2,1)S(1)}, bf16[64,4096]{1,0:T(8,128)(2,1)S(1)}, u32[]{:S(2)}, u32[]{:S(2)}) collective-permute-start(bf16[64,4096]{1,0:T(8,128)(2,1)S(1)} %collective-permute-done.1.refs_2_), channel_id=1, source_target_pairs={{0,10},{10,16},{16,26},{26,28},{28,22},{22,12},{12,6},{6,0},{2,4},... | collective-permute-start | bytes 1572872 | tf_op jit(solution)/shard_map/ppermute | solution.py:365
  15.8 11.2 %collective-permute-start.7 = (bf16[64,4096]{1,0:T(8,128)(2,1)S(1)}, bf16[64,4096]{1,0:T(8,128)(2,1)S(1)}, u32[]{:S(2)}, u32[]{:S(2)}) collective-permute-start(bf16[64,4096]{1,0:T(8,128)(2,1)S(1)} %collective-permute-done.3.refs_0_), channel_id=1, source_target_pairs={{0,10},{10,16},{16,26},{26,28},{28,22},{22,12},{12,6},{6,0},{2,4},... | collective-permute-start | bytes 1572872 | tf_op jit(solution)/shard_map/ppermute | solution.py:365
  21.4 11.2 %collective-permute-start.9 = (bf16[64,4096]{1,0:T(8,128)(2,1)S(1)}, bf16[64,4096]{1,0:T(8,128)(2,1)S(1)}, u32[]{:S(2)}, u32[]{:S(2)}) collective-permute-start(bf16[64,4096]{1,0:T(8,128)(2,1)S(1)} %collective-permute-done.5.refs_0_), channel_id=1, source_target_pairs={{0,10},{10,16},{16,26},{26,28},{28,22},{22,12},{12,6},{6,0},{2,4},... | collective-permute-start | bytes 1572872 | tf_op jit(solution)/shard_map/ppermute | solution.py:365
  23.5 11.2 %collective-permute-start.2 = (bf16[64,4096]{1,0:T(8,128)(2,1)S(1)}, bf16[64,4096]{1,0:T(8,128)(2,1)S(1)}, u32[]{:S(2)}, u32[]{:S(2)}) collective-permute-start(bf16[64,4096]{1,0:T(8,128)(2,1)S(1)} %collective-permute-done.1.refs_2_), channel_id=1, source_target_pairs={{0,2},{2,0},{4,6},{6,4},{8,10},{10,8},{12,14},{14,12},{16,18},{18,... | collective-permute-start | bytes 1572872 | tf_op jit(solution)/shard_map/ppermute | solution.py:369
  23.5 11.8 %collective-permute-start.4 = (bf16[64,4096]{1,0:T(8,128)(2,1)S(1)}, bf16[64,4096]{1,0:T(8,128)(2,1)S(1)}, u32[]{:S(2)}, u32[]{:S(2)}) collective-permute-start(bf16[64,4096]{1,0:T(8,128)(2,1)S(1)} %collective-permute-done.3.refs_0_), channel_id=1, source_target_pairs={{0,2},{2,0},{4,6},{6,4},{8,10},{10,8},{12,14},{14,12},{16,18},{18,... | collective-permute-start | bytes 1572872 | tf_op jit(solution)/shard_map/ppermute | solution.py:369
  27.0 12.9 %collective-permute-start.11 = (bf16[64,4096]{1,0:T(8,128)(2,1)S(1)}, bf16[64,4096]{1,0:T(8,128)(2,1)S(1)}, u32[]{:S(2)}, u32[]{:S(2)}) collective-permute-start(bf16[64,4096]{1,0:T(8,128)(2,1)S(1)} %collective-permute-done.7.refs_2_), channel_id=1, source_target_pairs={{0,10},{10,16},{16,26},{26,28},{28,22},{22,12},{12,6},{6,0},{2,4},... | collective-permute-start | bytes 1572872 | tf_op jit(solution)/shard_map/ppermute | solution.py:365
  32.6 11.2 %collective-permute-start.13 = (bf16[64,4096]{1,0:T(8,128)(2,1)S(1)}, bf16[64,4096]{1,0:T(8,128)(2,1)S(1)}, u32[]{:S(2)}, u32[]{:S(2)}) collective-permute-start(bf16[64,4096]{1,0:T(8,128)(2,1)S(1)} %collective-permute-done.9.refs_0_), channel_id=1, source_target_pairs={{0,10},{10,16},{16,26},{26,28},{28,22},{22,12},{12,6},{6,0},{2,4},... | collective-permute-start | bytes 1572872 | tf_op jit(solution)/shard_map/ppermute | solution.py:365
  34.8 14.1 %collective-permute-start.6 = (bf16[64,4096]{1,0:T(8,128)(2,1)S(1)}, bf16[64,4096]{1,0:T(8,128)(2,1)S(1)}, u32[]{:S(2)}, u32[]{:S(2)}) collective-permute-start(bf16[64,4096]{1,0:T(8,128)(2,1)S(1)} %collective-permute-done.5.refs_0_), channel_id=1, source_target_pairs={{0,2},{2,0},{4,6},{6,4},{8,10},{10,8},{12,14},{14,12},{16,18},{18,... | collective-permute-start | bytes 1572872 | tf_op jit(solution)/shard_map/ppermute | solution.py:369
  34.8 14.1 %collective-permute-start.8 = (bf16[64,4096]{1,0:T(8,128)(2,1)S(1)}, bf16[64,4096]{1,0:T(8,128)(2,1)S(1)}, u32[]{:S(2)}, u32[]{:S(2)}) collective-permute-start(bf16[64,4096]{1,0:T(8,128)(2,1)S(1)} %collective-permute-done.7.refs_2_), channel_id=1, source_target_pairs={{0,2},{2,0},{4,6},{6,4},{8,10},{10,8},{12,14},{14,12},{16,18},{18,... | collective-permute-start | bytes 1572872 | tf_op jit(solution)/shard_map/ppermute | solution.py:369
  35.3 16.2 %collective-permute-start.10 = (bf16[64,4096]{1,0:T(8,128)(2,1)S(1)}, bf16[64,4096]{1,0:T(8,128)(2,1)S(1)}, u32[]{:S(2)}, u32[]{:S(2)}) collective-permute-start(bf16[64,4096]{1,0:T(8,128)(2,1)S(1)} %collective-permute-done.9.refs_0_), channel_id=1, source_target_pairs={{0,2},{2,0},{4,6},{6,4},{8,10},{10,8},{12,14},{14,12},{16,18},{18,... | collective-permute-start | bytes 1572872 | tf_op jit(solution)/shard_map/ppermute | solution.py:369
  39.9 16.3 %collective-permute-start.12 = (bf16[64,4096]{1,0:T(8,128)(2,1)S(1)}, bf16[64,4096]{1,0:T(8,128)(2,1)S(1)}, u32[]{:S(2)}, u32[]{:S(2)}) collective-permute-start(bf16[64,4096]{1,0:T(8,128)(2,1)S(1)} %collective-permute-done.11.refs_0_), channel_id=1, source_target_pairs={{0,2},{2,0},{4,6},{6,4},{8,10},{10,8},{12,14},{14,12},{16,18},{18,... | collective-permute-start | bytes 1572872 | tf_op jit(solution)/shard_map/ppermute | solution.py:369
  43.9 16.9 %collective-permute-start.14 = (bf16[64,4096]{1,0:T(8,128)(2,1)S(1)}, bf16[64,4096]{1,0:T(8,128)(2,1)S(1)}, u32[]{:S(2)}, u32[]{:S(2)}) collective-permute-start(bf16[64,4096]{1,0:T(8,128)(2,1)S(1)} %collective-permute-done.13.refs_0_), channel_id=1, source_target_pairs={{0,2},{2,0},{4,6},{6,4},{8,10},{10,8},{12,14},{14,12},{16,18},{18,... | collective-permute-start | bytes 1572872 | tf_op jit(solution)/shard_map/ppermute | solution.py:369
  54.1 25.6 %collective-permute-start.17 = (bf16[1024,128]{1,0:T(8,128)(2,1)S(1)}, bf16[1024,128]{1,0:T(8,128)(2,1)S(1)}, u32[]{:S(2)}, u32[]{:S(2)}) collective-permute-start(bf16[1024,128]{1,0:T(8,128)(2,1)S(1)} %get-tuple-element.40), channel_id=1, source_target_pairs={{0,1},{1,0},{2,3},{3,2},{4,5},{5,4},{6,7},{7,6},{8,9},{9,8},{10,11... | collective-permute-start | bytes 786440 | tf_op jit(solution)/shard_map/ppermute | solution.py:361
  56.2 23.5 %collective-permute-start.16 = (bf16[1024,128]{1,0:T(8,128)(2,1)S(1)}, bf16[1024,128]{1,0:T(8,128)(2,1)S(1)}, u32[]{:S(2)}, u32[]{:S(2)}) collective-permute-start(bf16[1024,128]{1,0:T(8,128)(2,1)S(1)} %get-tuple-element.39), channel_id=1, source_target_pairs={{0,1},{1,0},{2,3},{3,2},{4,5},{5,4},{6,7},{7,6},{8,9},{9,8},{10,11... | collective-permute-start | bytes 786440 | tf_op jit(solution)/shard_map/ppermute | solution.py:361
  58.8 20.9 %copy-start.1 = (f32[1024]{0:T(1024)S(1)}, f32[1024]{0:T(1024)}, u32[]{:S(2)}) copy-start(f32[1024]{0:T(1024)} %param.5) | copy-start | bytes 12292
  58.8 20.9 %collective-permute-start.18 = (bf16[1024,128]{1,0:T(8,128)(2,1)S(1)}, bf16[1024,128]{1,0:T(8,128)(2,1)S(1)}, u32[]{:S(2)}, u32[]{:S(2)}) collective-permute-start(bf16[1024,128]{1,0:T(8,128)(2,1)S(1)} %get-tuple-element.41), channel_id=1, source_target_pairs={{0,1},{1,0},{2,3},{3,2},{4,5},{5,4},{6,7},{7,6},{8,9},{9,8},{10,11... | collective-permute-start | bytes 786440 | tf_op jit(solution)/shard_map/ppermute | solution.py:361
  63.3 17.9 %collective-permute-start.15 = (bf16[1024,128]{1,0:T(8,128)(2,1)S(1)}, bf16[1024,128]{1,0:T(8,128)(2,1)S(1)}, u32[]{:S(2)}, u32[]{:S(2)}) collective-permute-start(bf16[1024,128]{1,0:T(8,128)(2,1)S(1)} %get-tuple-element.38), channel_id=1, source_target_pairs={{0,1},{1,0},{2,3},{3,2},{4,5},{5,4},{6,7},{7,6},{8,9},{9,8},{10,11... | collective-permute-start | bytes 786440 | tf_op jit(solution)/shard_map/ppermute | solution.py:361
  63.4 16.3 %collective-permute-start.19 = (f32[8,128]{1,0:T(8,128)S(1)}, f32[8,128]{1,0:T(8,128)S(1)}, u32[]{:S(2)}, u32[]{:S(2)}) collective-permute-start(f32[8,128]{1,0:T(8,128)S(1)} %get-tuple-element.42.refs_3_), channel_id=1, source_target_pairs={{0,1},{1,0},{2,3},{3,2},{4,5},{5,4},{6,7},{7,6},{8,9},{9,8},{10,11... | collective-permute-start | bytes 12296 | tf_op jit(solution)/shard_map/ppermute | solution.py:361
  81.6 1.2 %collective-permute-start.20 = (f32[2,512]{1,0:T(2,128)S(1)}, f32[2,512]{1,0:T(2,128)S(1)}, u32[]{:S(2)}, u32[]{:S(2)}) collective-permute-start(f32[2,512]{1,0:T(2,128)S(1)} %get-tuple-element.46), channel_id=1, source_target_pairs={{0,2},{2,0},{4,6},{6,4},{8,10},{10,8},{12,14},{14,12},{16,18},{18,... | collective-permute-start | bytes 12296 | tf_op jit(solution)/shard_map/ppermute | solution.py:393
  82.9 3.1 %collective-permute-start.21 = (f32[2,512]{1,0:T(2,128)S(1)}, f32[2,512]{1,0:T(2,128)S(1)}, u32[]{:S(2)}, u32[]{:S(2)}) collective-permute-start(f32[2,512]{1,0:T(2,128)S(1)} %pad_maximum_fusion), channel_id=1, source_target_pairs={{0,6},{2,4},{4,2},{6,0},{8,14},{10,12},{12,10},{14,8},{16,22},{18,... | collective-permute-start | bytes 12296 | tf_op jit(solution)/shard_map/ppermute | solution.py:393
  86.0 3.1 %collective-permute-start.22 = (f32[2,512]{1,0:T(2,128)S(1)}, f32[2,512]{1,0:T(2,128)S(1)}, u32[]{:S(2)}, u32[]{:S(2)}) collective-permute-start(f32[2,512]{1,0:T(2,128)S(1)} %pad_maximum_fusion.1), channel_id=1, source_target_pairs={{0,10},{2,8},{4,14},{6,12},{8,2},{10,0},{12,6},{14,4},{16,26},{18,... | collective-permute-start | bytes 12296 | tf_op jit(solution)/shard_map/ppermute | solution.py:393
  89.1 4.0 %collective-permute-start.23 = (f32[2,512]{1,0:T(2,128)S(1)}, f32[2,512]{1,0:T(2,128)S(1)}, u32[]{:S(2)}, u32[]{:S(2)}) collective-permute-start(f32[2,512]{1,0:T(2,128)S(1)} %pad_maximum_fusion.2), channel_id=1, source_target_pairs={{0,18},{2,16},{4,22},{6,20},{8,26},{10,24},{12,30},{14,28},{16,2},... | collective-permute-start | bytes 12296 | tf_op jit(solution)/shard_map/ppermute | solution.py:393
